TPU v7x, 256 devices: a whole 4x4x8 slice. The times are simulated.
256 devices in a mesh: freq: 4 (over x_lo, core), rcv: 64 (over y, x_hi, z).
Axes of the slice: x: 4 (x_hi: 2, x_lo: 2; x = x_hi * 2 + x_lo), y: 4, z: 8, core: 2. Of those that a mesh axis runs over, the one named last changes fastest.
Arguments:
- spectra: bfloat16 [2, 128, 384, 8192], P(None, None, 'freq', 'rcv'), may hold values from -600 to 600
- valid: int32 [384, 8192], P(None, 'rcv'), may hold values from 0 to 1, as said below
- sources: int32 [256], P('rcv'), may hold values from 0 to 8191, as said below
- bounds: int32 [256, 8192, 2], P('freq', 'rcv'), may hold values from 0 to 128, as said below
Outputs:
- lag_corr: bfloat16 [256, 8192, 128], P('freq', 'rcv')
- peak_value: float32 [256, 8192], P('freq', 'rcv')
Inputs may be any that keep to these rules, and one draw needn't show every extreme that they name: `valid`: in each aligned group of 4 sub-windows at most one entry of a channel is 0. Source s is a channel from (s // 4) * 128 to (s // 4 + 1) * 128 - 1; the sources are distinct. bounds[s, c, 0] < bounds[s, c, 1] <= 128, and the window holds 16 to 64 lag samples.
All inputs are finite; a program needn't handle non-finite values.
Results may differ from a plain program's by a relative error of at most 0.007.
Values may be sent and summed in bfloat16 or wider, within the bound.
No kernel may reach another device: no remote copies, remote signals or barrier semaphores. Data moves between devices by JAX's collectives and lax.ppermute only.
A program may use at most 128 MiB of HBM per device.

v0:
```python
import functools
import math

import jax
import jax.numpy as jnp
import numpy as np
from jax import lax
from jax.experimental import pallas as pl
from jax.experimental.pallas import tpu as pltpu
from jax.sharding import Mesh, PartitionSpec as P

F = 128
F2 = F // 2
L = 128
W = 384
WB = 96
CH = 128
K2 = 4 * WB
NS = 16
MB = 1 << 20
COST = 10 ** 6
BF = jnp.bfloat16
F32 = jnp.float32
NT = (((1,), (1,)), ((), ()))


def shift(x, axis, step, size):
    return lax.ppermute(x, axis, [(k, (k + step) % size) for k in range(size)])


def pick_kernel(place_ref, spec_hbm, valid_ref, out_ref, spec_ref, raw_ref, sems):
    def fetch(g):
        bins = pl.ds(g * 16, 16)
        return pltpu.make_async_copy(spec_hbm.at[:, bins], spec_ref.at[:, bins], sems.at[g])

    for g in range(8):
        fetch(g).start()
    lane = lax.broadcasted_iota(jnp.int32, (8, CH), 1)
    row = lax.broadcasted_iota(jnp.int32, (8, CH), 0)
    hit = jnp.zeros((8, CH), F32)
    for k in range(4):
        hit = jnp.where((row == k) & (lane == place_ref[k]), 1.0, hit)
    onehot = hit.astype(BF)
    own_first = pl.multiple_of(place_ref[4] * WB, 8)

    def block(g, acc):
        fetch(g).wait()
        for j in range(8):
            k = 8 * g + j
            rows = jnp.concatenate([spec_ref[p, 2 * k + odd] for odd in range(2) for p in range(2)], axis=0)
            raw = lax.dot_general(onehot, rows, NT, preferred_element_type=F32)
            raw_ref[k] = raw
            acc = acc + raw * raw
        return acc

    acc = lax.fori_loop(0, 8, block, jnp.zeros((8, K2), F32))
    total = acc[:, 0:WB] + acc[:, WB:2 * WB] + acc[:, 2 * WB:3 * WB] + acc[:, 3 * WB:]
    picked_all = lax.dot_general(onehot, valid_ref[...].astype(BF), NT, preferred_element_type=F32)
    picked_own = lax.dot_general(onehot, valid_ref[pl.ds(own_first, WB), :].astype(BF), NT, preferred_element_type=F32)
    scale = picked_own / jnp.sqrt(total * (1.0 / F) + 1e-6)
    scale4 = jnp.concatenate([scale] * 4, axis=1)

    @pl.loop(0, F2)
    def _(k):
        out_ref[k] = (raw_ref[k] * scale4)[:4].astype(BF)

    out_ref[F2] = picked_all[:4].astype(BF)


VM = pl.BlockSpec(memory_space=pltpu.VMEM)


def pick(place, spectra, valid):
    return pl.pallas_call(
        pick_kernel,
        in_specs=[pl.BlockSpec(memory_space=pltpu.SMEM), pl.BlockSpec(memory_space=pltpu.HBM), VM],
        out_specs=VM,
        out_shape=jax.ShapeDtypeStruct((F2 + 1, 4, K2), BF),
        scratch_shapes=[pltpu.VMEM((2, F, WB, CH), BF), pltpu.VMEM((F2, 8, K2), F32), pltpu.SemaphoreType.DMA((8,))],
        compiler_params=pltpu.CompilerParams(vmem_limit_bytes=58 * MB),
        cost_estimate=pl.CostEstimate(flops=2 * 10 ** 9, bytes_accessed=7 * 10 ** 6, transcendentals=0),
        name="pick_sources",
    )(place, spectra, valid)


def whiten_kernel(spec_ref, valid_ref, out_ref):
    @pl.loop(0, WB // 16)
    def _(g):
        rows = pl.ds(pl.multiple_of(g * 16, 16), 16)

        def power(g, energy):
            for f in range(16):
                re = spec_ref[0, g * 16 + f, rows].astype(F32)
                im = spec_ref[1, g * 16 + f, rows].astype(F32)
                energy = energy + (re * re + im * im)
            return energy

        energy = lax.fori_loop(0, F // 16, power, jnp.zeros((16, CH), F32))
        scale = valid_ref[rows].astype(F32) / jnp.sqrt(energy * (1.0 / F) + 1e-6)

        @pl.loop(0, F // 16)
        def _(g):
            for f in range(16):
                for p in range(2):
                    out_ref[p, g * 16 + f, rows] = (spec_ref[p, g * 16 + f, rows].astype(F32) * scale).astype(BF)


def whiten(spectra, own_valid):
    return pl.pallas_call(
        whiten_kernel,
        in_specs=[VM, VM],
        out_specs=VM,
        out_shape=pltpu.VMEM((2, F, WB, CH), BF),
        compiler_params=pltpu.CompilerParams(vmem_limit_bytes=16 * MB),
        cost_estimate=pl.CostEstimate(flops=10 ** 6, bytes_accessed=10 ** 5, transcendentals=0),
        name="whiten_channels",
    )(spectra, own_valid)


def cross_kernel(n_ring, n_side, *refs):
    n_chunks = n_ring + n_side
    parts = refs[:n_chunks]
    valids = refs[n_chunks:2 * n_chunks]
    chan_ref, valid_ref, table_ref, keep_ref, send_ref, cnt_ref, x_ref = refs[2 * n_chunks:]
    step = pl.program_id(0)
    n = n_chunks * NS
    pad = jnp.zeros((256 - 2 * WB, 2 * CH), BF)
    held = []
    for k in range(8):
        lhs = jnp.concatenate([part[k] for part in parts], axis=0)
        for odd in range(2):
            re = chan_ref[0, step * 16 + 2 * k + odd]
            im = chan_ref[1, step * 16 + 2 * k + odd]
            top = jnp.concatenate([re, im], axis=1)
            low = jnp.concatenate([im, -re], axis=1)
            if odd:
                rhs = jnp.concatenate([pad, top, low], axis=0)
                used = lhs[:, 128:]
            else:
                rhs = jnp.concatenate([top, low, pad], axis=0)
                used = lhs[:, :256]
            both = jnp.dot(used, rhs, preferred_element_type=F32)
            held.append(both.astype(BF))
    for p in range(2):
        block = jnp.stack([h[:, p * CH:(p + 1) * CH] for h in held])
        first_bin = pl.multiple_of(p * F + step * 16, 16)
        x_ref[:, pl.ds(first_bin, 16), :] = jnp.transpose(block, (1, 0, 2))

    @pl.when(step == 7)
    def _():
        for c in range(n_chunks):
            cnt_ref[c * NS:(c + 1) * NS] = jnp.dot(valids[c][0], valid_ref[...], preferred_element_type=F32)
        table = table_ref[...]

        def pair(out_ref, slot, row):
            lag = jnp.dot(table, jnp.concatenate([x_ref[row], x_ref[row + 1]], axis=1), preferred_element_type=F32)
            out_ref[slot] = lag[:, :CH].astype(BF)
            out_ref[slot + 1] = lag[:, CH:].astype(BF)

        for block, (out_ref, half) in enumerate(((keep_ref, 0), (keep_ref, 1), (send_ref, 0), (send_ref, 1))):
            for c in range(n_ring):
                for q in range(0, NS // 4, 2):
                    pair(out_ref, half * (n_ring * 4) + c * 4 + q, c * NS + block * 4 + q)

        if n_side:
            for q in range(0, n_side * NS, 2):
                pair(send_ref, n_ring * 8 + q, n_ring * NS + q)


def cross(ring, side, chan, valid, table):
    chunks = list(ring) + list(side)
    n_ring, n_side, n_chunks = len(ring), len(side), len(chunks)
    n = n_chunks * NS
    part = pl.BlockSpec((8, NS, K2), lambda i: (i, 0, 0))
    tail = pl.BlockSpec((1, NS, K2), lambda i: (F2, 0, 0))
    sizes = [n_ring * 8, n_ring * 8 + n_side * NS]
    return pl.pallas_call(
        functools.partial(cross_kernel, n_ring, n_side),
        grid=(8,),
        in_specs=[part] * n_chunks + [tail] * n_chunks + [
            VM,
            pl.BlockSpec((W, CH), lambda i: (0, 0)),
            pl.BlockSpec((L, 2 * F), lambda i: (0, 0)),
        ],
        out_specs=[pl.BlockSpec((k, L, CH), lambda i: (0, 0, 0)) for k in sizes] + [pl.BlockSpec((n, CH), lambda i: (0, 0))],
        out_shape=[jax.ShapeDtypeStruct((k, L, CH), BF) for k in sizes] + [jax.ShapeDtypeStruct((n, CH), F32)],
        scratch_shapes=[pltpu.VMEM((n, 2 * F, CH), BF)],
        compiler_params=pltpu.CompilerParams(vmem_limit_bytes=24 * MB),
        cost_estimate=pl.CostEstimate(flops=COST * n_chunks, bytes_accessed=10 ** 5 * n_chunks, transcendentals=0),
        name="cross_lag",
    )(*chunks, *chunks, chan, valid, table)


def finish_kernel(rows_ref, live_ref, bounds_ref, *refs):
    n_in = len(refs) - 2
    lag_ref, peak_ref = refs[n_in], refs[n_in + 1]
    lag_index = lax.broadcasted_iota(jnp.int32, (L, CH), 0)
    first = 0
    for g in range(n_in // 3):
        keep_ref, recv_ref, cnt_ref = refs[3 * g], refs[3 * g + 1], refs[3 * g + 2]
        count = recv_ref.shape[0]

        def one(r, keep_ref=keep_ref, recv_ref=recv_ref, cnt_ref=cnt_ref, first=first):
            row = rows_ref[first + r]
            total = keep_ref[r].astype(F32) + recv_ref[r].astype(F32)
            value = (total / cnt_ref[pl.ds(r, 1), :]).astype(BF)
            lag_ref[row] = value.T
            lower = bounds_ref[0, pl.ds(row, 1), :]
            upper = bounds_ref[1, pl.ds(row, 1), :]
            inside = (lag_index >= lower) & (lag_index < upper)
            best = jnp.max(jnp.where(inside, value.astype(F32), -jnp.inf), axis=0, keepdims=True)
            peak_ref[pl.ds(row, 1), :] = best

        @pl.when(live_ref[g] != 0)
        def _(one=one, count=count):
            @pl.loop(0, count // 4)
            def _(q):
                for k in range(4):
                    one(q * 4 + k)
        first += count


def finish(rows, live, bounds2, groups):
    flat = [x for g in groups for x in g]
    smem = pl.BlockSpec(memory_space=pltpu.SMEM)
    return pl.pallas_call(
        finish_kernel,
        in_specs=[smem, smem] + [VM] * (1 + len(flat)),
        out_specs=[VM, VM],
        out_shape=[jax.ShapeDtypeStruct((64, CH, L), BF), jax.ShapeDtypeStruct((64, CH), F32)],
        compiler_params=pltpu.CompilerParams(vmem_limit_bytes=24 * MB),
        cost_estimate=pl.CostEstimate(flops=10 ** 7, bytes_accessed=8 * 10 ** 6, transcendentals=0),
        name="finish_lags",
    )(rows, live, bounds2, *flat)


def lag_table():
    bins_col = (1 + jnp.arange(F, dtype=jnp.int32))[:, None]
    lag_row = jnp.arange(L, dtype=jnp.int32)[None, :] - L // 2
    angles = (bins_col * lag_row % (2 * F)).astype(F32) * (2.0 * math.pi / (2 * F))
    cos, sin = jnp.cos(angles).astype(BF), jnp.sin(angles).astype(BF)
    return jnp.concatenate([cos, -sin], axis=0).T


def tie(values):
    return lax.optimization_barrier(values)


def add(a, b):
    return (a.astype(F32) + b.astype(F32)).astype(BF)


def local(spectra, valid, sources, bounds):
    xlo = lax.axis_index("xlo")
    core = lax.axis_index("core")
    y = lax.axis_index("y")
    xh = lax.axis_index("xh")
    z = lax.axis_index("z")
    freq = xlo * 2 + core
    offsets = sources - ((y * 2 + xh) * 8 + z) * CH
    place = jnp.concatenate([offsets, freq[None].astype(jnp.int32)])
    valid_b = valid.astype(BF)
    own_valid = lax.dynamic_slice_in_dim(valid_b, freq * WB, WB, 0)
    table = lag_table()

    picked = pick(place, spectra, valid)
    other = shift(picked, "xh", 1, 2)
    mine1 = jnp.concatenate([picked[:, :2], other[:, :2]], axis=1)
    mine2 = jnp.concatenate([picked[:, 2:], other[:, 2:]], axis=1)

    def swap_core(keep, send):
        got = shift(send, "core", 1, 2)
        n, half = keep.shape[0], keep.shape[0] // 2
        side = add(send[n:], got[n:]) if send.shape[0] > n else None
        return add(keep[:half], got[:half]), add(keep[half:], got[half:n]), side

    def swap_x(mine, away):
        return mine, shift(away, "xlo", 1, 2)

    def side_x(total, odd, low_is_mine):
        half = total.shape[0] // 2
        pairs = [((h * 2 + c) * 4 + k, ((1 - h) * 2 + c) * 4 + k)
                 for k in range(4) for c in range(2) for h in range(2) if c == (k + odd) % 2]
        mine = jnp.where(low_is_mine, total[:half], total[half:])
        away = jnp.where(low_is_mine, total[half:], total[:half])
        return mine, lax.ppermute(away, ("xlo", "core", "y"), pairs)

    r = (freq - y) % 4
    halves = ((0, 1, -1, 2), (-2, 3, -3, 4))

    def lanes(ks, first):
        return [(k, e, first + j) for k in ks for e in range(2) for j in range(2)]

    spots = []
    for ks in ((0, 1, -1), (2, -2), (3, -3, 4)):
        spots += lanes(ks, 0)
    spots += lanes(halves[0], 2) + lanes(halves[1], 2)
    one = spots + lanes(halves[0], 2) + lanes(halves[1], 2)
    two = spots + lanes(halves[1], 2) + lanes(halves[0], 2)
    tables = np.array([one, two], np.int32)
    spot = jnp.where(r == 1, tables[0], tables[1])
    rows = ((xh ^ spot[:, 1]) * 32 + ((z + spot[:, 0]) % 8) * 4 + spot[:, 2]).astype(jnp.int32)
    even = 1 - r % 2
    live = jnp.where(np.arange(6) < 3, 1, jnp.where(np.arange(6) == 3, even, 1 - even)).astype(jnp.int32)
    bounds2 = jnp.stack([bounds[:, :, 0], bounds[:, :, 1]])

    r1 = (shift(mine1, "y", -1, 4), shift(mine1, "y", 2, 4), shift(mine1, "y", 1, 4))
    b1, bm1 = shift(mine2, "z", -1, 8), shift(mine2, "z", 1, 8)
    b2, bm2 = shift(b1, "z", -1, 8), shift(bm1, "z", 1, 8)
    b3, bm3 = shift(b2, "z", -1, 8), shift(bm2, "z", 1, 8)
    up, far, down = r1
    by_y = jnp.stack([mine1, up, far, down])
    order = [lax.dynamic_index_in_dim(by_y, ((freq ^ m) - y) % 4, 0, keepdims=False) for m in (0, 2, 1, 3)]
    a0 = jnp.concatenate(order, axis=1)
    h0 = [jnp.concatenate([mine2, b1, bm1, b2], axis=1)]
    a0, h0, bm2, b3, bm3, rows, live = tie((a0, h0, bm2, b3, bm3, rows, live))
    chan = whiten(spectra, own_valid)

    def run(ring, side=(), after=()):
        gated = tie((table,) + tuple(after))[0] if after else table
        return cross(ring, side, chan, valid_b, gated)

    a1, am1 = shift(a0, "z", -1, 8), shift(a0, "z", 1, 8)
    h0.append(shift(h0[0], "y", -1, 4))
    b4 = shift(b3, "z", -1, 8)
    h1 = [jnp.concatenate([bm2, b3, bm3, b4], axis=1)]
    h1.append(shift(h1[0], "y", 1, 4))
    a1, am1, h0, h1, chan = tie((a1, am1, h0, h1, chan))
    a2, am2 = shift(a1, "z", -1, 8), shift(am1, "z", 1, 8)
    h0.append(shift(h0[1], "y", -1, 4))
    h1.append(shift(h1[1], "y", 1, 4))
    keep1, send1, cnt1 = run([a0, a1, am1], [h0[1], h1[1]])
    a2, am2, h0, h1, keep1, send1 = tie((a2, am2, h0, h1, keep1, send1))
    a3, am3 = shift(a2, "z", -1, 8), shift(am2, "z", 1, 8)
    h0.append(shift(h0[2], "y", -1, 4))
    h1.append(shift(h1[2], "y", 1, 4))
    mine1, away1, side1 = swap_core(keep1, send1)
    keep2, send2, cnt2 = run([a2, am2], [h0[0], h1[0], h0[2], h1[2]], (side1,))
    k1 = swap_x(mine1, away1)
    a3, am3, h0, h1, k1, side1, keep2, send2 = tie((a3, am3, h0, h1, k1, side1, keep2, send2))
    p1 = side_x(side1, 1, r == 1)
    mine2, away2, side2 = swap_core(keep2, send2)
    cut = F2 // 2
    a4 = jnp.concatenate([shift(am3[:cut], "z", 1, 8), shift(a3[cut:], "z", -1, 8)], axis=0)
    a4, p1, mine2, away2, side2 = tie((a4, p1, mine2, away2, side2))
    p0 = side_x(side2, 0, r == 0)
    k2 = swap_x(mine2, away2)
    keep3, send3, cnt3 = run([a3, am3, a4], [h0[3], h1[3]])
    mine3, away3, side3 = swap_core(keep3, send3)
    p3 = side_x(side3, 1, r == 3)
    k3 = swap_x(mine3, away3)

    groups = []
    for ks, (mine, recv), cnt in ((3, k1, cnt1), (2, k2, cnt2), (3, k3, cnt3)):
        groups.append((mine, recv, jnp.concatenate([cnt[c * NS:c * NS + 4] for c in range(ks)], axis=0)))
    cnt1, cnt2, cnt3 = cnt1[3 * NS:], cnt2[2 * NS:], cnt3[3 * NS:]
    groups.append((*p0, jnp.where(r == 0, cnt2[:2 * NS], cnt2[2 * NS:])))
    groups.append((*p1, jnp.where(r == 1, cnt1[:NS], cnt1[NS:])))
    groups.append((*p3, jnp.where(r == 3, cnt3[:NS], cnt3[NS:])))
    lag_corr, peak = finish(rows, live, bounds2, groups)
    return (lag_corr, peak)


def solution(mesh):
    fine = Mesh(mesh.devices.reshape(2, 2, 4, 2, 8), ("xlo", "core", "y", "xh", "z"))
    freq, rcv = ("xlo", "core"), ("y", "xh", "z")
    in_specs = (P(None, None, freq, rcv), P(None, rcv), P(rcv), P(freq, rcv, None))
    out_specs = (P(freq, rcv, None), P(freq, rcv))
    return jax.shard_map(local, mesh=fine, in_specs=in_specs, out_specs=out_specs, check_vma=False)
```

profile of v0, /device:TPU:1, one launch (start us, length us, event | category | flops | bytes accessed | tf_op | source)
XLA Modules:
  0.0 183.2 jit_solution(14679409769580145184)
XLA Ops:
  0.6 0.7 broadcast_subtract_fusion
  1.3 0.6 pad_add_fusion.1.place_ref
  1.9 6.7 %pick_sources.1 = bf16[65,4,384]{2,1,0:T(4,128)(2,1)} custom-call(s32[5]{0:T(128)} %pad_add_fusion.1.place_ref, bf16[2,128,96,128]{3,2,1,0:T(8,128)(2,1)} %spec_ref.1, s32[384,128]{1,0:T(8,128)} %valid_ref.1), custom_call_target="tpu_custom_call" | custom-call | flops 2000000000 | bytes 7000000 | tf_op jit(solution)/shard_map/pick_sources/pallas_call | solution.py:74
  8.6 3.7 %collective-permute-start = (bf16[65,4,384]{2,1,0:T(4,128)(2,1)}, bf16[65,4,384]{2,1,0:T(4,128)(2,1)S(1)}, u32[]{:S(2)}, u32[]{:S(2)}) collective-permute-start(bf16[65,4,384]{2,1,0:T(4,128)(2,1)} %pick_sources.1), channel_id=1, source_target_pairs={{0,8},{8,0},{1,9},{9,1},{2,10},{10,2},{3,11},{11,3},{4,12},{12,4},... | collective-permute-start | bytes 599048 | tf_op jit(solution)/shard_map/ppermute | solution.py:28
  12.3 1.2 fusion.10
  13.5 2.7 %collective-permute-done = bf16[65,4,384]{2,1,0:T(4,128)(2,1)S(1)} collective-permute-done((bf16[65,4,384]{2,1,0:T(4,128)(2,1)}, bf16[65,4,384]{2,1,0:T(4,128)(2,1)S(1)}, u32[]{:S(2)}, u32[]{:S(2)}) %collective-permute-start) | collective-permute-done | bytes 199712 | tf_op jit(solution)/shard_map/ppermute | solution.py:28
  16.4 0.2 pad_maximum_fusion.5
  16.6 6.5 %collective-permute-start.4 = (bf16[65,4,384]{2,1,0:T(4,128)(2,1)S(1)}, bf16[65,4,384]{2,1,0:T(4,128)(2,1)S(1)}, u32[]{:S(2)}, u32[]{:S(2)}) collective-permute-start(bf16[65,4,384]{2,1,0:T(4,128)(2,1)S(1)} %pad_maximum_fusion.5), channel_id=1, source_target_pairs={{0,7},{1,0},{2,1},{3,2},{4,3},{5,4},{6,5},{7,6},{8,15},{9,8},{10,9... | collective-permute-start | bytes 599048 | tf_op jit(solution)/shard_map/ppermute | solution.py:28
  23.1 0.2 fusion.8
  23.4 2.8 %collective-permute-start.1 = (bf16[65,4,384]{2,1,0:T(4,128)(2,1)S(1)}, bf16[65,4,384]{2,1,0:T(4,128)(2,1)S(1)}, u32[]{:S(2)}, u32[]{:S(2)}) collective-permute-start(bf16[65,4,384]{2,1,0:T(4,128)(2,1)S(1)} %get-tuple-element.117), channel_id=1, source_target_pairs={{0,48},{16,0},{32,16},{48,32},{1,49},{17,1},{33,17},{49,33},{2,50}... | collective-permute-start | bytes 599048 | tf_op jit(solution)/shard_map/ppermute | solution.py:28
  26.2 0.3 collective-permute-start.2
  26.5 0.7 collective-permute-start.3
  27.2 2.7 %collective-permute-start.6 = (bf16[65,4,384]{2,1,0:T(4,128)(2,1)S(1)}, bf16[65,4,384]{2,1,0:T(4,128)(2,1)}, u32[]{:S(2)}, u32[]{:S(2)}) collective-permute-start(bf16[65,4,384]{2,1,0:T(4,128)(2,1)S(1)} %collective-permute-done.4), channel_id=1, source_target_pairs={{0,7},{1,0},{2,1},{3,2},{4,3},{5,4},{6,5},{7,6},{8,15},{9,8},{10,9... | collective-permute-start | bytes 599048 | tf_op jit(solution)/shard_map/ppermute | solution.py:28
  30.0 0.8 collective-permute-done.1
  30.8 1.5 collective-permute-done.2
  32.3 5.9 %collective-permute-done.3 = bf16[65,4,384]{2,1,0:T(4,128)(2,1)S(1)} collective-permute-done((bf16[65,4,384]{2,1,0:T(4,128)(2,1)S(1)}, bf16[65,4,384]{2,1,0:T(4,128)(2,1)S(1)}, u32[]{:S(2)}, u32[]{:S(2)}) %collective-permute-start.3) | collective-permute-done | bytes 199712 | tf_op jit(solution)/shard_map/ppermute | solution.py:28
  38.3 0.7 pad_maximum_fusion
  39.0 2.5 %collective-permute-start.8 = (bf16[65,4,384]{2,1,0:T(4,128)(2,1)}, bf16[65,4,384]{2,1,0:T(4,128)(2,1)}, u32[]{:S(2)}, u32[]{:S(2)}) collective-permute-start(bf16[65,4,384]{2,1,0:T(4,128)(2,1)} %collective-permute-done.6), channel_id=1, source_target_pairs={{0,7},{1,0},{2,1},{3,2},{4,3},{5,4},{6,5},{7,6},{8,15},{9,8},{10,9... | collective-permute-start | bytes 599048 | tf_op jit(solution)/shard_map/ppermute | solution.py:28
  41.5 0.3 dynamic-slice_bitcast_fusion.3
  41.8 0.6 pad_maximum_fusion.1.refs_0_.refs_5_
  42.4 3.5 %concatenate.38.refs_2_.refs_8_ = bf16[65,16,384]{2,1,0:T(8,128)(2,1)S(1)} concatenate(bf16[65,2,384]{2,1,0:T(2,128)(2,1)S(1)} %get-tuple-element.114, bf16[65,2,384]{2,1,0:T(2,128)(2,1)S(1)} %get-tuple-element.112, bf16[65,4,384]{2,1,0:T(4,128)(2,1)S(1)} %collective-permute-done.4, bf16[65,4,384]{2,1,0:T(4,128)(2,1)S(1)} %collective-permute-done.5, ...), dimensions={1} | concatenate | bytes 1597440 | tf_op jit(solution)/shard_map/concatenate | solution.py:315
  45.9 1.5 collective-permute-done.9
  47.3 1.3 collective-permute-start.13
  48.7 1.4 collective-permute-start.11
  50.1 2.0 %collective-permute-done.13 = bf16[65,4,384]{2,1,0:T(4,128)(2,1)S(1)} collective-permute-done((bf16[65,4,384]{2,1,0:T(4,128)(2,1)}, bf16[65,4,384]{2,1,0:T(4,128)(2,1)S(1)}, u32[]{:S(2)}, u32[]{:S(2)}) %collective-permute-start.13) | collective-permute-done | bytes 199712 | tf_op jit(solution)/shard_map/ppermute | solution.py:28
  52.1 1.6 pad_maximum_fusion.2.refs_3_.refs_9_
  53.8 0.9 convert_element_type.95.refs_11_.refs_13_
  54.8 2.8 %copy-done = bf16[2,128,96,128]{3,2,1,0:T(8,128)(2,1)S(1)} copy-done((bf16[2,128,96,128]{3,2,1,0:T(8,128)(2,1)S(1)}, bf16[2,128,96,128]{3,2,1,0:T(8,128)(2,1)}, u32[]{:S(2)}) %copy-start) | copy-done | bytes 6291480
  57.5 2.9 %whiten_channels.1.refs_10_.refs_12_ = bf16[2,128,96,128]{3,2,1,0:T(8,128)(2,1)S(1)} custom-call(bf16[2,128,96,128]{3,2,1,0:T(8,128)(2,1)S(1)} %copy-done, bf16[96,128]{1,0:T(8,128)(2,1)S(1)} %constant_dynamic-slice_fusion.valid_ref), custom_call_target="tpu_custom_call" | custom-call | flops 1000000 | bytes 100000 | tf_op jit(solution)/shard_map/whiten_channels/pallas_call | solution.py:109
  60.4 8.0 %collective-permute-done.10.refs_1_.refs_6_ = bf16[65,16,384]{2,1,0:T(8,128)(2,1)S(1)} collective-permute-done((bf16[65,16,384]{2,1,0:T(8,128)(2,1)S(1)}, bf16[65,16,384]{2,1,0:T(8,128)(2,1)S(1)}, u32[]{:S(2)}, u32[]{:S(2)}) %collective-permute-start.10) | collective-permute-done | bytes 798752 | tf_op jit(solution)/shard_map/ppermute | solution.py:28
  68.4 3.5 %collective-permute-start.15 = (bf16[65,16,384]{2,1,0:T(8,128)(2,1)S(1)}, bf16[65,16,384]{2,1,0:T(8,128)(2,1)S(1)}, u32[]{:S(2)}, u32[]{:S(2)}) collective-permute-start(bf16[65,16,384]{2,1,0:T(8,128)(2,1)S(1)} %collective-permute-done.10.refs_1_.refs_6_), channel_id=1, source_target_pairs={{0,7},{1,0},{2,1},{3,2},{4,3},{5,4},{6,5},{7,6},{8,15},{9,8},{10,9... | collective-permute-start | bytes 2396168 | tf_op jit(solution)/shard_map/ppermute | solution.py:28
  71.9 1.5 collective-permute-start.18
  73.4 0.3 cosine_convert_fusion
  73.7 0.3 fusion.3
  74.1 8.0 %cross_lag.3 = (bf16[24,128,128]{2,1,0:T(8,128)(2,1)S(1)}, bf16[56,128,128]{2,1,0:T(8,128)(2,1)S(1)}, f32[80,128]{1,0:T(8,128)S(1)}) custom-call(bf16[65,16,384]{2,1,0:T(8,128)(2,1)S(1)} %pad_maximum_fusion.1.refs_0_.refs_5_, bf16[65,16,384]{2,1,0:T(8,128)(2,1)S(1)} %collective-permute-done.10.refs_1_.refs_6_, ...), custom_call_target="tpu_custom_call" | custom-call | flops 5000000 | bytes 500000 | tf_op jit(solution)/shard_map/cross_lag/pallas_call | solution.py:177
  82.1 1.1 collective-permute-done.15.refs_0_.refs_6_
  83.2 3.3 %collective-permute-done.16.refs_1_.refs_7_ = bf16[65,16,384]{2,1,0:T(8,128)(2,1)S(1)} collective-permute-done((bf16[65,16,384]{2,1,0:T(8,128)(2,1)}, bf16[65,16,384]{2,1,0:T(8,128)(2,1)S(1)}, u32[]{:S(2)}, u32[]{:S(2)}) %collective-permute-start.16) | collective-permute-done | bytes 798752 | tf_op jit(solution)/shard_map/ppermute | solution.py:28
  86.5 7.1 %collective-permute-start.23 = (bf16[56,128,128]{2,1,0:T(8,128)(2,1)S(1)}, bf16[56,128,128]{2,1,0:T(8,128)(2,1)S(1)}, u32[]{:S(2)}, u32[]{:S(2)}) collective-permute-start(bf16[56,128,128]{2,1,0:T(8,128)(2,1)S(1)} %get-tuple-element.72), channel_id=1, source_target_pairs={{0,64},{64,0},{1,65},{65,1},{2,66},{66,2},{3,67},{67,3},{4,68},{68... | collective-permute-start | bytes 5505032 | tf_op jit(solution)/shard_map/ppermute | solution.py:28
  93.6 2.7 %collective-permute-start.19 = (bf16[65,16,384]{2,1,0:T(8,128)(2,1)S(1)}, bf16[65,16,384]{2,1,0:T(8,128)(2,1)S(1)}, u32[]{:S(2)}, u32[]{:S(2)}) collective-permute-start(bf16[65,16,384]{2,1,0:T(8,128)(2,1)S(1)} %collective-permute-done.15.refs_0_.refs_6_), channel_id=1, source_target_pairs={{0,7},{1,0},{2,1},{3,2},{4,3},{5,4},{6,5},{7,6},{8,15},{9,8},{10,9... | collective-permute-start | bytes 2396168 | tf_op jit(solution)/shard_map/ppermute | solution.py:28
  96.3 1.5 collective-permute-start.22
  97.7 0.2 add_convert_fusion.5
  98.0 1.5 collective-permute-start.24
  99.4 0.4 add_convert_fusion.2
  99.8 6.1 %cross_lag.4 = (bf16[16,128,128]{2,1,0:T(8,128)(2,1)S(1)}, bf16[80,128,128]{2,1,0:T(8,128)(2,1)S(1)}, f32[96,128]{1,0:T(8,128)S(1)}) custom-call(bf16[65,16,384]{2,1,0:T(8,128)(2,1)S(1)} %collective-permute-done.15.refs_0_.refs_6_, bf16[65,16,384]{2,1,0:T(8,128)(2,1)S(1)} %collective-permute-done.16.refs_1_.refs_7_, ...), custom_call_target="tpu_custom_call" | custom-call | flops 6000000 | bytes 600000 | tf_op jit(solution)/shard_map/cross_lag/pallas_call | solution.py:177
  106.0 7.5 %collective-permute-done.19.refs_0_.refs_5_ = bf16[65,16,384]{2,1,0:T(8,128)(2,1)S(1)} collective-permute-done((bf16[65,16,384]{2,1,0:T(8,128)(2,1)S(1)}, bf16[65,16,384]{2,1,0:T(8,128)(2,1)S(1)}, u32[]{:S(2)}, u32[]{:S(2)}) %collective-permute-start.19) | collective-permute-done | bytes 798752 | tf_op jit(solution)/shard_map/ppermute | solution.py:28
  113.5 3.1 %collective-permute-done.20.refs_1_.refs_6_ = bf16[65,16,384]{2,1,0:T(8,128)(2,1)S(1)} collective-permute-done((bf16[65,16,384]{2,1,0:T(8,128)(2,1)S(1)}, bf16[65,16,384]{2,1,0:T(8,128)(2,1)S(1)}, u32[]{:S(2)}, u32[]{:S(2)}) %collective-permute-start.20) | collective-permute-done | bytes 798752 | tf_op jit(solution)/shard_map/ppermute | solution.py:28
  116.6 1.2 collective-permute-start.28
  117.8 2.7 %collective-permute-start.26 = (bf16[33,16,384]{2,1,0:T(8,128)(2,1)S(1)}, bf16[33,16,384]{2,1,0:T(8,128)(2,1)S(1)}, u32[]{:S(2)}, u32[]{:S(2)}) collective-permute-start(bf16[33,16,384]{2,1,0:T(8,128)(2,1)S(1)} %slice.181), channel_id=1, source_target_pairs={{0,7},{1,0},{2,1},{3,2},{4,3},{5,4},{6,5},{7,6},{8,15},{9,8},{10,9... | collective-permute-start | bytes 1216520 | tf_op jit(solution)/shard_map/ppermute | solution.py:28
  120.7 3.1 %collective-permute-start.27 = (bf16[16,128,128]{2,1,0:T(8,128)(2,1)S(1)}, bf16[16,128,128]{2,1,0:T(8,128)(2,1)S(1)}, u32[]{:S(2)}, u32[]{:S(2)}) collective-permute-start(bf16[16,128,128]{2,1,0:T(8,128)(2,1)S(1)} %get-tuple-element.106), channel_id=1, source_target_pairs={{64,192},{192,64},{16,144},{144,16},{96,224},{224,96},{48,176},{17... | collective-permute-start | bytes 1572872 | tf_op jit(solution)/shard_map/ppermute | solution.py:286
  123.8 8.5 %collective-permute-done.25 = bf16[32,16,384]{2,1,0:T(8,128)(2,1)S(1)} collective-permute-done((bf16[32,16,384]{2,1,0:T(8,128)(2,1)S(1)}, bf16[32,16,384]{2,1,0:T(8,128)(2,1)S(1)}, u32[]{:S(2)}, u32[]{:S(2)}) %collective-permute-start.25) | collective-permute-done | bytes 393248 | tf_op jit(solution)/shard_map/ppermute | solution.py:28
  132.4 0.9 add_convert_fusion.7
  133.2 2.1 %add_convert_fusion = bf16[64,128,128]{2,1,0:T(8,128)(2,1)} fusion(bf16[80,128,128]{2,1,0:T(8,128)(2,1)S(1)} %collective-permute-done.28, bf16[80,128,128]{2,1,0:T(8,128)(2,1)S(1)} %get-tuple-element.83), kind=kLoop, calls=%fused_computation | loop fusion | flops 4194304 | bytes 6291456 | tf_op jit(solution)/shard_map/convert_element_type | solution.py:250
  135.3 6.8 %cross_lag.5 = (bf16[24,128,128]{2,1,0:T(8,128)(2,1)S(1)}, bf16[56,128,128]{2,1,0:T(8,128)(2,1)}, f32[80,128]{1,0:T(8,128)S(1)}) custom-call(bf16[65,16,384]{2,1,0:T(8,128)(2,1)S(1)} %collective-permute-done.19.refs_0_.refs_5_, bf16[65,16,384]{2,1,0:T(8,128)(2,1)S(1)} %collective-permute-done.20.refs_1_.refs_6_, ...), custom_call_target="tpu_custom_call" | custom-call | flops 5000000 | bytes 500000 | tf_op jit(solution)/shard_map/cross_lag/pallas_call | solution.py:177
  142.1 1.1 collective-permute-start.30
  143.4 1.7 broadcast_select_fusion
  145.0 0.7 collective-permute-start.32
  145.8 1.2 collective-permute-done.30
  147.0 1.9 %add_convert_fusion.1 = bf16[32,128,128]{2,1,0:T(8,128)(2,1)S(1)} fusion(bf16[56,128,128]{2,1,0:T(8,128)(2,1)} %collective-permute-done.30, bf16[56,128,128]{2,1,0:T(8,128)(2,1)} %get-tuple-element.91), kind=kLoop, calls=%fused_computation.1 | loop fusion | flops 2097152 | bytes 3145728 | tf_op jit(solution)/shard_map/convert_element_type | solution.py:250
  149.0 3.1 %collective-permute-start.33 = (bf16[16,128,128]{2,1,0:T(8,128)(2,1)S(1)}, bf16[16,128,128]{2,1,0:T(8,128)(2,1)S(1)}, u32[]{:S(2)}, u32[]{:S(2)}) collective-permute-start(bf16[16,128,128]{2,1,0:T(8,128)(2,1)S(1)} %get-tuple-element.104), channel_id=1, source_target_pairs={{64,192},{192,64},{16,144},{144,16},{96,224},{224,96},{48,176},{17... | collective-permute-start | bytes 1572872 | tf_op jit(solution)/shard_map/ppermute | solution.py:286
  152.0 1.3 add_convert_fusion.3
  153.4 0.4 collective-permute-start.31
  153.8 1.1 collective-permute-start.29
  154.9 24.0 %collective-permute-done.29.refs_4_ = bf16[8,128,128]{2,1,0:T(8,128)(2,1)S(1)} collective-permute-done((bf16[8,128,128]{2,1,0:T(8,128)(2,1)S(1)}, bf16[8,128,128]{2,1,0:T(8,128)(2,1)S(1)}, u32[]{:S(2)}, u32[]{:S(2)}) %collective-permute-start.29) | collective-permute-done | bytes 262176 | tf_op jit(solution)/shard_map/ppermute | solution.py:28
  178.9 4.3 %finish_lags.1 = (bf16[64,128,128]{2,1,0:T(8,128)(2,1)}, f32[64,128]{1,0:T(8,128)}) custom-call(s32[96]{0:T(128)S(1)} %fusion.6.rows_ref, s32[6]{0:T(128)S(1)} %select_select_fusion.live_ref, s32[2,64,128]{2,1,0:T(8,128)S(1)} %pad_add_fusion.bounds_ref, bf16[12,128,128]{2,1,0:T(8,128)(2,1)S(1)} %get-tuple-element.76.refs_0_, ...), custom_call_target="tpu_custom_call" | custom-call | flops 10000000 | bytes 8000000 | tf_op jit(solution)/shard_map/finish_lags/pallas_call | solution.py:226
  (67 shorter events, 1.0 us)
Async XLA Ops:
  1.9 11.6 %copy-start.3 = (s32[96,3]{0,1:T(4,128)S(1)}, s32[96,3]{0,1:T(4,128)}, u32[]{:S(2)}) copy-start(s32[96,3]{0,1:T(4,128)} %constant.122.clone) | copy-start | bytes 3460
  1.9 11.6 %copy-start.4 = (s32[96,3]{0,1:T(4,128)S(1)}, s32[96,3]{0,1:T(4,128)}, u32[]{:S(2)}) copy-start(s32[96,3]{0,1:T(4,128)} %constant.123.clone) | copy-start | bytes 3460
  8.6 21.3 %copy-start.5 = (pred[6]{0:T(512)(128)(4,1)S(1)}, pred[6]{0:T(512)(128)(4,1)}, u32[]{:S(2)}) copy-start(pred[6]{0:T(512)(128)(4,1)} %constant.124.clone) | copy-start | bytes 22
  8.6 21.3 %copy-start.6 = (pred[6]{0:T(512)(128)(4,1)S(1)}, pred[6]{0:T(512)(128)(4,1)}, u32[]{:S(2)}) copy-start(pred[6]{0:T(512)(128)(4,1)} %constant.125.clone) | copy-start | bytes 22
  8.6 7.6 %collective-permute-start = (bf16[65,4,384]{2,1,0:T(4,128)(2,1)}, bf16[65,4,384]{2,1,0:T(4,128)(2,1)S(1)}, u32[]{:S(2)}, u32[]{:S(2)}) collective-permute-start(bf16[65,4,384]{2,1,0:T(4,128)(2,1)} %pick_sources.1), channel_id=1, source_target_pairs={{0,8},{8,0},{1,9},{9,1},{2,10},{10,2},{3,11},{11,3},{4,12},{12,4},... | collective-permute-start | bytes 599048 | tf_op jit(solution)/shard_map/ppermute | solution.py:28
  16.6 10.6 %collective-permute-start.4 = (bf16[65,4,384]{2,1,0:T(4,128)(2,1)S(1)}, bf16[65,4,384]{2,1,0:T(4,128)(2,1)S(1)}, u32[]{:S(2)}, u32[]{:S(2)}) collective-permute-start(bf16[65,4,384]{2,1,0:T(4,128)(2,1)S(1)} %pad_maximum_fusion.5), channel_id=1, source_target_pairs={{0,7},{1,0},{2,1},{3,2},{4,3},{5,4},{6,5},{7,6},{8,15},{9,8},{10,9... | collective-permute-start | bytes 599048 | tf_op jit(solution)/shard_map/ppermute | solution.py:28
  23.1 6.8 %collective-permute-start.5 = (bf16[65,4,384]{2,1,0:T(4,128)(2,1)S(1)}, bf16[65,4,384]{2,1,0:T(4,128)(2,1)S(1)}, u32[]{:S(2)}, u32[]{:S(2)}) collective-permute-start(bf16[65,4,384]{2,1,0:T(4,128)(2,1)S(1)} %pad_maximum_fusion.5), channel_id=1, source_target_pairs={{0,1},{1,2},{2,3},{3,4},{4,5},{5,6},{6,7},{7,0},{8,9},{9,10},{10,1... | collective-permute-start | bytes 599048 | tf_op jit(solution)/shard_map/ppermute | solution.py:28
  23.4 7.4 %collective-permute-start.1 = (bf16[65,4,384]{2,1,0:T(4,128)(2,1)S(1)}, bf16[65,4,384]{2,1,0:T(4,128)(2,1)S(1)}, u32[]{:S(2)}, u32[]{:S(2)}) collective-permute-start(bf16[65,4,384]{2,1,0:T(4,128)(2,1)S(1)} %get-tuple-element.117), channel_id=1, source_target_pairs={{0,48},{16,0},{32,16},{48,32},{1,49},{17,1},{33,17},{49,33},{2,50}... | collective-permute-start | bytes 599048 | tf_op jit(solution)/shard_map/ppermute | solution.py:28
  26.2 6.2 %collective-permute-start.2 = (bf16[65,4,384]{2,1,0:T(4,128)(2,1)S(1)}, bf16[65,4,384]{2,1,0:T(4,128)(2,1)S(1)}, u32[]{:S(2)}, u32[]{:S(2)}) collective-permute-start(bf16[65,4,384]{2,1,0:T(4,128)(2,1)S(1)} %get-tuple-element.117), channel_id=1, source_target_pairs={{0,32},{16,48},{32,0},{48,16},{1,33},{17,49},{33,1},{49,17},{2,34}... | collective-permute-start | bytes 599048 | tf_op jit(solution)/shard_map/ppermute | solution.py:28
  26.5 11.7 %collective-permute-start.3 = (bf16[65,4,384]{2,1,0:T(4,128)(2,1)S(1)}, bf16[65,4,384]{2,1,0:T(4,128)(2,1)S(1)}, u32[]{:S(2)}, u32[]{:S(2)}) collective-permute-start(bf16[65,4,384]{2,1,0:T(4,128)(2,1)S(1)} %get-tuple-element.117), channel_id=1, source_target_pairs={{0,16},{16,32},{32,48},{48,0},{1,17},{17,33},{33,49},{49,1},{2,18}... | collective-permute-start | bytes 599048 | tf_op jit(solution)/shard_map/ppermute | solution.py:28
  27.2 11.8 %collective-permute-start.6 = (bf16[65,4,384]{2,1,0:T(4,128)(2,1)S(1)}, bf16[65,4,384]{2,1,0:T(4,128)(2,1)}, u32[]{:S(2)}, u32[]{:S(2)}) collective-permute-start(bf16[65,4,384]{2,1,0:T(4,128)(2,1)S(1)} %collective-permute-done.4), channel_id=1, source_target_pairs={{0,7},{1,0},{2,1},{3,2},{4,3},{5,4},{6,5},{7,6},{8,15},{9,8},{10,9... | collective-permute-start | bytes 599048 | tf_op jit(solution)/shard_map/ppermute | solution.py:28
  29.9 11.6 %collective-permute-start.7 = (bf16[65,4,384]{2,1,0:T(4,128)(2,1)S(1)}, bf16[65,4,384]{2,1,0:T(4,128)(2,1)S(1)}, u32[]{:S(2)}, u32[]{:S(2)}) collective-permute-start(bf16[65,4,384]{2,1,0:T(4,128)(2,1)S(1)} %collective-permute-done.5), channel_id=1, source_target_pairs={{0,1},{1,2},{2,3},{3,4},{4,5},{5,6},{6,7},{7,0},{8,9},{9,10},{10,1... | collective-permute-start | bytes 599048 | tf_op jit(solution)/shard_map/ppermute | solution.py:28
  39.0 6.9 %collective-permute-start.8 = (bf16[65,4,384]{2,1,0:T(4,128)(2,1)}, bf16[65,4,384]{2,1,0:T(4,128)(2,1)}, u32[]{:S(2)}, u32[]{:S(2)}) collective-permute-start(bf16[65,4,384]{2,1,0:T(4,128)(2,1)} %collective-permute-done.6), channel_id=1, source_target_pairs={{0,7},{1,0},{2,1},{3,2},{4,3},{5,4},{6,5},{7,6},{8,15},{9,8},{10,9... | collective-permute-start | bytes 599048 | tf_op jit(solution)/shard_map/ppermute | solution.py:28
  41.5 5.9 %collective-permute-start.9 = (bf16[65,4,384]{2,1,0:T(4,128)(2,1)S(1)}, bf16[65,4,384]{2,1,0:T(4,128)(2,1)}, u32[]{:S(2)}, u32[]{:S(2)}) collective-permute-start(bf16[65,4,384]{2,1,0:T(4,128)(2,1)S(1)} %collective-permute-done.7), channel_id=1, source_target_pairs={{0,1},{1,2},{2,3},{3,4},{4,5},{5,6},{6,7},{7,0},{8,9},{9,10},{10,1... | collective-permute-start | bytes 599048 | tf_op jit(solution)/shard_map/ppermute | solution.py:28
  47.3 4.8 %collective-permute-start.13 = (bf16[65,4,384]{2,1,0:T(4,128)(2,1)}, bf16[65,4,384]{2,1,0:T(4,128)(2,1)S(1)}, u32[]{:S(2)}, u32[]{:S(2)}) collective-permute-start(bf16[65,4,384]{2,1,0:T(4,128)(2,1)} %collective-permute-done.8), channel_id=1, source_target_pairs={{0,7},{1,0},{2,1},{3,2},{4,3},{5,4},{6,5},{7,6},{8,15},{9,8},{10,9... | collective-permute-start | bytes 599048 | tf_op jit(solution)/shard_map/ppermute | solution.py:28
  48.6 19.8 %collective-permute-start.10 = (bf16[65,16,384]{2,1,0:T(8,128)(2,1)S(1)}, bf16[65,16,384]{2,1,0:T(8,128)(2,1)S(1)}, u32[]{:S(2)}, u32[]{:S(2)}) collective-permute-start(bf16[65,16,384]{2,1,0:T(8,128)(2,1)S(1)} %pad_maximum_fusion.1.refs_0_.refs_5_), channel_id=1, source_target_pairs={{0,7},{1,0},{2,1},{3,2},{4,3},{5,4},{6,5},{7,6},{8,15},{9,8},{10,9... | collective-permute-start | bytes 2396168 | tf_op jit(solution)/shard_map/ppermute | solution.py:28
  48.7 19.7 %collective-permute-start.11 = (bf16[65,16,384]{2,1,0:T(8,128)(2,1)S(1)}, bf16[65,16,384]{2,1,0:T(8,128)(2,1)}, u32[]{:S(2)}, u32[]{:S(2)}) collective-permute-start(bf16[65,16,384]{2,1,0:T(8,128)(2,1)S(1)} %pad_maximum_fusion.1.refs_0_.refs_5_), channel_id=1, source_target_pairs={{0,1},{1,2},{2,3},{3,4},{4,5},{5,6},{6,7},{7,0},{8,9},{9,10},{10,1... | collective-permute-start | bytes 2396168 | tf_op jit(solution)/shard_map/ppermute | solution.py:28
  50.1 18.3 %collective-permute-start.12 = (bf16[65,16,384]{2,1,0:T(8,128)(2,1)S(1)}, bf16[65,16,384]{2,1,0:T(8,128)(2,1)}, u32[]{:S(2)}, u32[]{:S(2)}) collective-permute-start(bf16[65,16,384]{2,1,0:T(8,128)(2,1)S(1)} %concatenate.38.refs_2_.refs_8_), channel_id=1, source_target_pairs={{0,48},{16,0},{32,16},{48,32},{1,49},{17,1},{33,17},{49,33},{2,50}... | collective-permute-start | bytes 2396168 | tf_op jit(solution)/shard_map/ppermute | solution.py:28
  53.7 14.7 %collective-permute-start.14 = (bf16[65,16,384]{2,1,0:T(8,128)(2,1)S(1)}, bf16[65,16,384]{2,1,0:T(8,128)(2,1)}, u32[]{:S(2)}, u32[]{:S(2)}) collective-permute-start(bf16[65,16,384]{2,1,0:T(8,128)(2,1)S(1)} %pad_maximum_fusion.2.refs_3_.refs_9_), channel_id=1, source_target_pairs={{0,16},{16,32},{32,48},{48,0},{1,17},{17,33},{33,49},{49,1},{2,18}... | collective-permute-start | bytes 2396168 | tf_op jit(solution)/shard_map/ppermute | solution.py:28
  54.7 2.8 %copy-start = (bf16[2,128,96,128]{3,2,1,0:T(8,128)(2,1)S(1)}, bf16[2,128,96,128]{3,2,1,0:T(8,128)(2,1)}, u32[]{:S(2)}) copy-start(bf16[2,128,96,128]{3,2,1,0:T(8,128)(2,1)} %spec_ref.1) | copy-start | bytes 18874372
  68.4 14.8 %collective-permute-start.15 = (bf16[65,16,384]{2,1,0:T(8,128)(2,1)S(1)}, bf16[65,16,384]{2,1,0:T(8,128)(2,1)S(1)}, u32[]{:S(2)}, u32[]{:S(2)}) collective-permute-start(bf16[65,16,384]{2,1,0:T(8,128)(2,1)S(1)} %collective-permute-done.10.refs_1_.refs_6_), channel_id=1, source_target_pairs={{0,7},{1,0},{2,1},{3,2},{4,3},{5,4},{6,5},{7,6},{8,15},{9,8},{10,9... | collective-permute-start | bytes 2396168 | tf_op jit(solution)/shard_map/ppermute | solution.py:28
  71.9 14.6 %collective-permute-start.16 = (bf16[65,16,384]{2,1,0:T(8,128)(2,1)}, bf16[65,16,384]{2,1,0:T(8,128)(2,1)S(1)}, u32[]{:S(2)}, u32[]{:S(2)}) collective-permute-start(bf16[65,16,384]{2,1,0:T(8,128)(2,1)} %collective-permute-done.11.refs_2_.refs_7_), channel_id=1, source_target_pairs={{0,1},{1,2},{2,3},{3,4},{4,5},{5,6},{6,7},{7,0},{8,9},{9,10},{10,1... | collective-permute-start | bytes 2396168 | tf_op jit(solution)/shard_map/ppermute | solution.py:28
  71.9 14.6 %collective-permute-start.17 = (bf16[65,16,384]{2,1,0:T(8,128)(2,1)}, bf16[65,16,384]{2,1,0:T(8,128)(2,1)S(1)}, u32[]{:S(2)}, u32[]{:S(2)}) collective-permute-start(bf16[65,16,384]{2,1,0:T(8,128)(2,1)} %collective-permute-done.12.refs_3_.refs_8_), channel_id=1, source_target_pairs={{0,48},{16,0},{32,16},{48,32},{1,49},{17,1},{33,17},{49,33},{2,50}... | collective-permute-start | bytes 2396168 | tf_op jit(solution)/shard_map/ppermute | solution.py:28
  71.9 14.6 %collective-permute-start.18 = (bf16[65,16,384]{2,1,0:T(8,128)(2,1)}, bf16[65,16,384]{2,1,0:T(8,128)(2,1)S(1)}, u32[]{:S(2)}, u32[]{:S(2)}) collective-permute-start(bf16[65,16,384]{2,1,0:T(8,128)(2,1)} %collective-permute-done.14.refs_4_.refs_9_), channel_id=1, source_target_pairs={{0,16},{16,32},{32,48},{48,0},{1,17},{17,33},{33,49},{49,1},{2,18}... | collective-permute-start | bytes 2396168 | tf_op jit(solution)/shard_map/ppermute | solution.py:28
  86.5 11.2 %collective-permute-start.23 = (bf16[56,128,128]{2,1,0:T(8,128)(2,1)S(1)}, bf16[56,128,128]{2,1,0:T(8,128)(2,1)S(1)}, u32[]{:S(2)}, u32[]{:S(2)}) collective-permute-start(bf16[56,128,128]{2,1,0:T(8,128)(2,1)S(1)} %get-tuple-element.72), channel_id=1, source_target_pairs={{0,64},{64,0},{1,65},{65,1},{2,66},{66,2},{3,67},{67,3},{4,68},{68... | collective-permute-start | bytes 5505032 | tf_op jit(solution)/shard_map/ppermute | solution.py:28
  93.6 19.9 %collective-permute-start.19 = (bf16[65,16,384]{2,1,0:T(8,128)(2,1)S(1)}, bf16[65,16,384]{2,1,0:T(8,128)(2,1)S(1)}, u32[]{:S(2)}, u32[]{:S(2)}) collective-permute-start(bf16[65,16,384]{2,1,0:T(8,128)(2,1)S(1)} %collective-permute-done.15.refs_0_.refs_6_), channel_id=1, source_target_pairs={{0,7},{1,0},{2,1},{3,2},{4,3},{5,4},{6,5},{7,6},{8,15},{9,8},{10,9... | collective-permute-start | bytes 2396168 | tf_op jit(solution)/shard_map/ppermute | solution.py:28
  96.3 20.3 %collective-permute-start.20 = (bf16[65,16,384]{2,1,0:T(8,128)(2,1)S(1)}, bf16[65,16,384]{2,1,0:T(8,128)(2,1)S(1)}, u32[]{:S(2)}, u32[]{:S(2)}) collective-permute-start(bf16[65,16,384]{2,1,0:T(8,128)(2,1)S(1)} %collective-permute-done.16.refs_1_.refs_7_), channel_id=1, source_target_pairs={{0,1},{1,2},{2,3},{3,4},{4,5},{5,6},{6,7},{7,0},{8,9},{9,10},{10,1... | collective-permute-start | bytes 2396168 | tf_op jit(solution)/shard_map/ppermute | solution.py:28
  96.3 20.3 %collective-permute-start.21 = (bf16[65,16,384]{2,1,0:T(8,128)(2,1)S(1)}, bf16[65,16,384]{2,1,0:T(8,128)(2,1)S(1)}, u32[]{:S(2)}, u32[]{:S(2)}) collective-permute-start(bf16[65,16,384]{2,1,0:T(8,128)(2,1)S(1)} %collective-permute-done.17.refs_4_.refs_10_), channel_id=1, source_target_pairs={{0,48},{16,0},{32,16},{48,32},{1,49},{17,1},{33,17},{49,33},{2,50}... | collective-permute-start | bytes 2396168 | tf_op jit(solution)/shard_map/ppermute | solution.py:28
  96.3 20.3 %collective-permute-start.22 = (bf16[65,16,384]{2,1,0:T(8,128)(2,1)S(1)}, bf16[65,16,384]{2,1,0:T(8,128)(2,1)S(1)}, u32[]{:S(2)}, u32[]{:S(2)}) collective-permute-start(bf16[65,16,384]{2,1,0:T(8,128)(2,1)S(1)} %collective-permute-done.18.refs_5_.refs_11_), channel_id=1, source_target_pairs={{0,16},{16,32},{32,48},{48,0},{1,17},{17,33},{33,49},{49,1},{2,18}... | collective-permute-start | bytes 2396168 | tf_op jit(solution)/shard_map/ppermute | solution.py:28
  98.0 18.6 %collective-permute-start.24 = (bf16[12,128,128]{2,1,0:T(8,128)(2,1)S(1)}, bf16[12,128,128]{2,1,0:T(8,128)(2,1)S(1)}, u32[]{:S(2)}, u32[]{:S(2)}) collective-permute-start(bf16[12,128,128]{2,1,0:T(8,128)(2,1)S(1)} %get-tuple-element.100), channel_id=1, source_target_pairs={{0,128},{128,0},{1,129},{129,1},{2,130},{130,2},{3,131},{131,3},{4... | collective-permute-start | bytes 1179656 | tf_op jit(solution)/shard_map/ppermute | solution.py:28
  116.6 15.8 %collective-permute-start.28 = (bf16[80,128,128]{2,1,0:T(8,128)(2,1)S(1)}, bf16[80,128,128]{2,1,0:T(8,128)(2,1)S(1)}, u32[]{:S(2)}, u32[]{:S(2)}) collective-permute-start(bf16[80,128,128]{2,1,0:T(8,128)(2,1)S(1)} %get-tuple-element.83), channel_id=1, source_target_pairs={{0,64},{64,0},{1,65},{65,1},{2,66},{66,2},{3,67},{67,3},{4,68},{68... | collective-permute-start | bytes 7864328 | tf_op jit(solution)/shard_map/ppermute | solution.py:28
  117.8 14.4 %collective-permute-start.26 = (bf16[33,16,384]{2,1,0:T(8,128)(2,1)S(1)}, bf16[33,16,384]{2,1,0:T(8,128)(2,1)S(1)}, u32[]{:S(2)}, u32[]{:S(2)}) collective-permute-start(bf16[33,16,384]{2,1,0:T(8,128)(2,1)S(1)} %slice.181), channel_id=1, source_target_pairs={{0,7},{1,0},{2,1},{3,2},{4,3},{5,4},{6,5},{7,6},{8,15},{9,8},{10,9... | collective-permute-start | bytes 1216520 | tf_op jit(solution)/shard_map/ppermute | solution.py:28
  120.5 11.7 %collective-permute-start.25 = (bf16[32,16,384]{2,1,0:T(8,128)(2,1)S(1)}, bf16[32,16,384]{2,1,0:T(8,128)(2,1)S(1)}, u32[]{:S(2)}, u32[]{:S(2)}) collective-permute-start(bf16[32,16,384]{2,1,0:T(8,128)(2,1)S(1)} %slice.180), channel_id=1, source_target_pairs={{0,1},{1,2},{2,3},{3,4},{4,5},{5,6},{6,7},{7,0},{8,9},{9,10},{10,1... | collective-permute-start | bytes 1179656 | tf_op jit(solution)/shard_map/ppermute | solution.py:28
  120.7 14.6 %collective-permute-start.27 = (bf16[16,128,128]{2,1,0:T(8,128)(2,1)S(1)}, bf16[16,128,128]{2,1,0:T(8,128)(2,1)S(1)}, u32[]{:S(2)}, u32[]{:S(2)}) collective-permute-start(bf16[16,128,128]{2,1,0:T(8,128)(2,1)S(1)} %get-tuple-element.106), channel_id=1, source_target_pairs={{64,192},{192,64},{16,144},{144,16},{96,224},{224,96},{48,176},{17... | collective-permute-start | bytes 1572872 | tf_op jit(solution)/shard_map/ppermute | solution.py:286
  135.3 7.9 %copy-start.2 = (s32[64,128,2]{1,2,0:T(2,128)S(1)}, s32[64,128,2]{1,2,0:T(2,128)}, u32[]{:S(2)}) copy-start(s32[64,128,2]{1,2,0:T(2,128)} %param.11) | copy-start | bytes 196612
  142.1 4.9 %collective-permute-start.30 = (bf16[56,128,128]{2,1,0:T(8,128)(2,1)}, bf16[56,128,128]{2,1,0:T(8,128)(2,1)}, u32[]{:S(2)}, u32[]{:S(2)}) collective-permute-start(bf16[56,128,128]{2,1,0:T(8,128)(2,1)} %get-tuple-element.91), channel_id=1, source_target_pairs={{0,64},{64,0},{1,65},{65,1},{2,66},{66,2},{3,67},{67,3},{4,68},{68... | collective-permute-start | bytes 5505032 | tf_op jit(solution)/shard_map/ppermute | solution.py:28
  145.0 33.9 %collective-permute-start.32 = (bf16[32,128,128]{2,1,0:T(8,128)(2,1)S(1)}, bf16[32,128,128]{2,1,0:T(8,128)(2,1)S(1)}, u32[]{:S(2)}, u32[]{:S(2)}) collective-permute-start(bf16[32,128,128]{2,1,0:T(8,128)(2,1)S(1)} %get-tuple-element.102), channel_id=1, source_target_pairs={{0,128},{128,0},{80,208},{208,80},{32,160},{160,32},{112,240},{240... | collective-permute-start | bytes 3145736 | tf_op jit(solution)/shard_map/ppermute | solution.py:286
  148.9 4.9 %copy-start.1 = (bf16[8,128,128]{2,1,0:T(8,128)(2,1)S(1)}, bf16[8,128,128]{2,1,0:T(8,128)(2,1)}, u32[]{:S(2)}) copy-start(bf16[8,128,128]{2,1,0:T(8,128)(2,1)} %get-tuple-element.85) | copy-start | bytes 786436
  149.0 30.0 %collective-permute-start.33 = (bf16[16,128,128]{2,1,0:T(8,128)(2,1)S(1)}, bf16[16,128,128]{2,1,0:T(8,128)(2,1)S(1)}, u32[]{:S(2)}, u32[]{:S(2)}) collective-permute-start(bf16[16,128,128]{2,1,0:T(8,128)(2,1)S(1)} %get-tuple-element.104), channel_id=1, source_target_pairs={{64,192},{192,64},{16,144},{144,16},{96,224},{224,96},{48,176},{17... | collective-permute-start | bytes 1572872 | tf_op jit(solution)/shard_map/ppermute | solution.py:286
  153.4 25.5 %collective-permute-start.31 = (bf16[12,128,128]{2,1,0:T(8,128)(2,1)S(1)}, bf16[12,128,128]{2,1,0:T(8,128)(2,1)S(1)}, u32[]{:S(2)}, u32[]{:S(2)}) collective-permute-start(bf16[12,128,128]{2,1,0:T(8,128)(2,1)S(1)} %get-tuple-element.98), channel_id=1, source_target_pairs={{0,128},{128,0},{1,129},{129,1},{2,130},{130,2},{3,131},{131,3},{4... | collective-permute-start | bytes 1179656 | tf_op jit(solution)/shard_map/ppermute | solution.py:28
  153.8 25.1 %collective-permute-start.29 = (bf16[8,128,128]{2,1,0:T(8,128)(2,1)S(1)}, bf16[8,128,128]{2,1,0:T(8,128)(2,1)S(1)}, u32[]{:S(2)}, u32[]{:S(2)}) collective-permute-start(bf16[8,128,128]{2,1,0:T(8,128)(2,1)S(1)} %copy-done.1), channel_id=1, source_target_pairs={{0,128},{128,0},{1,129},{129,1},{2,130},{130,2},{3,131},{131,3},{4... | collective-permute-start | bytes 786440 | tf_op jit(solution)/shard_map/ppermute | solution.py:28
where the time goes:
time: 185 us; the launch traced here: 183 us
  waiting for transfers between devices  71.1 us (38%)
  starting transfers between devices  53.1 us (29%)
  Pallas kernels  34.7 us (19%)
  other arithmetic  15 us (8%)
  local copies, waits for them, and re-layouts  8.12 us (4%)
    ppermute x31, waiting for transfers between devices, shift(): return lax.ppermute(x, axis, [(k, (k + step) % size) for k in range(size)])  71.1 us
    ppermute x31, starting transfers between devices, shift(): return lax.ppermute(x, axis, [(k, (k + step) % size) for k in range(size)])  46.3 us
    pallas_call x3, Pallas kernels, cross(): pl.pallas_call(functools.partial(cross_kernel, n_ring, n_side), grid=(8,)...  20.9 us
    ppermute x3, starting transfers between devices, side_x(): return (mine, lax.ppermute(away, ('xlo', 'core', 'y'), pairs))  6.85 us
    convert_element_type x6, other arithmetic, add(): return (a.astype(F32) + b.astype(F32)).astype(BF)  6.81 us
    pallas_call x1, Pallas kernels, pick(): pl.pallas_call(pick_kernel, in_specs=[pl.BlockSpec(memory_space=pltpu.SME...  6.66 us
    pallas_call x1, Pallas kernels, finish(): pl.pallas_call(finish_kernel, in_specs=[smem, smem] + [VM] * (1 + len(fla...  4.28 us
  transfers between devices with their start and end apart: 34, of which 14 were waited for; matrix products, arithmetic and copies ran while one was open for 10% of the time, Pallas kernels for 9%

commit v1 on v0

--- a/solution.py
+++ b/solution.py
@@ -342,9 +342,9 @@
     mine2, away2, side2 = swap_core(keep2, send2)
     cut = F2 // 2
     a4 = jnp.concatenate([shift(am3[:cut], "z", 1, 8), shift(a3[cut:], "z", -1, 8)], axis=0)
-    a4, p1, mine2, away2, side2 = tie((a4, p1, mine2, away2, side2))
+    k2 = swap_x(mine2, away2)
+    a4, p1, k2, side2 = tie((a4, p1, k2, side2))
     p0 = side_x(side2, 0, r == 0)
-    k2 = swap_x(mine2, away2)
     keep3, send3, cnt3 = run([a3, am3, a4], [h0[3], h1[3]])
     mine3, away3, side3 = swap_core(keep3, send3)
     p3 = side_x(side3, 1, r == 3)

time: 185 us -> 184 us (level)
  transfers between devices with their start and end apart: 34 -> 34, of which waited for: 14 -> 15; matrix products, arithmetic and copies ran while one was open for 10% -> 10% of each run, Pallas kernels for 9% -> 9%
where the time goes in v1:
time: 184 us; the launch traced here: 182 us
  waiting for transfers between devices  70.1 us (38%)
  starting transfers between devices  54.1 us (29%)
  Pallas kernels  34.7 us (19%)
  other arithmetic  14.3 us (8%)
  local copies, waits for them, and re-layouts  8.11 us (4%)
    ppermute x31, waiting for transfers between devices, shift(): return lax.ppermute(x, axis, [(k, (k + step) % size) for k in range(size)])  70 us
    ppermute x31, starting transfers between devices, shift(): return lax.ppermute(x, axis, [(k, (k + step) % size) for k in range(size)])  47.3 us
    pallas_call x3, Pallas kernels, cross(): pl.pallas_call(functools.partial(cross_kernel, n_ring, n_side), grid=(8,)...  20.9 us
    ppermute x3, starting transfers between devices, side_x(): return (mine, lax.ppermute(away, ('xlo', 'core', 'y'), pairs))  6.85 us
    pallas_call x1, Pallas kernels, pick(): pl.pallas_call(pick_kernel, in_specs=[pl.BlockSpec(memory_space=pltpu.SME...  6.66 us
    convert_element_type x6, other arithmetic, add(): return (a.astype(F32) + b.astype(F32)).astype(BF)  6.09 us
    pallas_call x1, Pallas kernels, finish(): pl.pallas_call(finish_kernel, in_specs=[smem, smem] + [VM] * (1 + len(fla...  4.26 us
  transfers between devices with their start and end apart: 34, of which 15 were waited for; matrix products, arithmetic and copies ran while one was open for 10% of the time, Pallas kernels for 9%

profile of v1, /device:TPU:1, one launch (start us, length us, event | category | flops | bytes accessed | tf_op | source)
XLA Modules:
  0.0 182.5 jit_solution(9606879979084944191)
XLA Ops:
  0.6 0.7 broadcast_subtract_fusion
  1.3 0.6 pad_add_fusion.1.place_ref
  2.0 6.7 %pick_sources.1 = bf16[65,4,384]{2,1,0:T(4,128)(2,1)} custom-call(s32[5]{0:T(128)} %pad_add_fusion.1.place_ref, bf16[2,128,96,128]{3,2,1,0:T(8,128)(2,1)} %spec_ref.1, s32[384,128]{1,0:T(8,128)} %valid_ref.1), custom_call_target="tpu_custom_call" | custom-call | flops 2000000000 | bytes 7000000 | tf_op jit(solution)/shard_map/pick_sources/pallas_call | solution.py:74
  8.7 3.7 %collective-permute-start = (bf16[65,4,384]{2,1,0:T(4,128)(2,1)}, bf16[65,4,384]{2,1,0:T(4,128)(2,1)S(1)}, u32[]{:S(2)}, u32[]{:S(2)}) collective-permute-start(bf16[65,4,384]{2,1,0:T(4,128)(2,1)} %pick_sources.1), channel_id=1, source_target_pairs={{0,8},{8,0},{1,9},{9,1},{2,10},{10,2},{3,11},{11,3},{4,12},{12,4},... | collective-permute-start | bytes 599048 | tf_op jit(solution)/shard_map/ppermute | solution.py:28
  12.3 1.2 fusion.10
  13.6 2.7 %collective-permute-done = bf16[65,4,384]{2,1,0:T(4,128)(2,1)S(1)} collective-permute-done((bf16[65,4,384]{2,1,0:T(4,128)(2,1)}, bf16[65,4,384]{2,1,0:T(4,128)(2,1)S(1)}, u32[]{:S(2)}, u32[]{:S(2)}) %collective-permute-start) | collective-permute-done | bytes 199712 | tf_op jit(solution)/shard_map/ppermute | solution.py:28
  16.4 0.2 pad_maximum_fusion.5
  16.6 6.5 %collective-permute-start.4 = (bf16[65,4,384]{2,1,0:T(4,128)(2,1)S(1)}, bf16[65,4,384]{2,1,0:T(4,128)(2,1)S(1)}, u32[]{:S(2)}, u32[]{:S(2)}) collective-permute-start(bf16[65,4,384]{2,1,0:T(4,128)(2,1)S(1)} %pad_maximum_fusion.5), channel_id=1, source_target_pairs={{0,7},{1,0},{2,1},{3,2},{4,3},{5,4},{6,5},{7,6},{8,15},{9,8},{10,9... | collective-permute-start | bytes 599048 | tf_op jit(solution)/shard_map/ppermute | solution.py:28
  23.2 0.2 fusion.8
  23.4 2.8 %collective-permute-start.1 = (bf16[65,4,384]{2,1,0:T(4,128)(2,1)S(1)}, bf16[65,4,384]{2,1,0:T(4,128)(2,1)S(1)}, u32[]{:S(2)}, u32[]{:S(2)}) collective-permute-start(bf16[65,4,384]{2,1,0:T(4,128)(2,1)S(1)} %get-tuple-element.117), channel_id=1, source_target_pairs={{0,48},{16,0},{32,16},{48,32},{1,49},{17,1},{33,17},{49,33},{2,50}... | collective-permute-start | bytes 599048 | tf_op jit(solution)/shard_map/ppermute | solution.py:28
  26.2 0.3 collective-permute-start.2
  26.6 0.7 collective-permute-start.3
  27.3 2.7 %collective-permute-start.6 = (bf16[65,4,384]{2,1,0:T(4,128)(2,1)S(1)}, bf16[65,4,384]{2,1,0:T(4,128)(2,1)}, u32[]{:S(2)}, u32[]{:S(2)}) collective-permute-start(bf16[65,4,384]{2,1,0:T(4,128)(2,1)S(1)} %collective-permute-done.4), channel_id=1, source_target_pairs={{0,7},{1,0},{2,1},{3,2},{4,3},{5,4},{6,5},{7,6},{8,15},{9,8},{10,9... | collective-permute-start | bytes 599048 | tf_op jit(solution)/shard_map/ppermute | solution.py:28
  30.1 0.8 collective-permute-done.1
  30.8 1.5 collective-permute-done.2
  32.4 5.9 %collective-permute-done.3 = bf16[65,4,384]{2,1,0:T(4,128)(2,1)S(1)} collective-permute-done((bf16[65,4,384]{2,1,0:T(4,128)(2,1)S(1)}, bf16[65,4,384]{2,1,0:T(4,128)(2,1)S(1)}, u32[]{:S(2)}, u32[]{:S(2)}) %collective-permute-start.3) | collective-permute-done | bytes 199712 | tf_op jit(solution)/shard_map/ppermute | solution.py:28
  38.3 0.7 pad_maximum_fusion
  39.0 2.5 %collective-permute-start.8 = (bf16[65,4,384]{2,1,0:T(4,128)(2,1)}, bf16[65,4,384]{2,1,0:T(4,128)(2,1)}, u32[]{:S(2)}, u32[]{:S(2)}) collective-permute-start(bf16[65,4,384]{2,1,0:T(4,128)(2,1)} %collective-permute-done.6), channel_id=1, source_target_pairs={{0,7},{1,0},{2,1},{3,2},{4,3},{5,4},{6,5},{7,6},{8,15},{9,8},{10,9... | collective-permute-start | bytes 599048 | tf_op jit(solution)/shard_map/ppermute | solution.py:28
  41.5 0.3 dynamic-slice_bitcast_fusion.3
  41.8 0.6 pad_maximum_fusion.1.refs_0_.refs_5_
  42.4 3.5 %concatenate.38.refs_2_.refs_8_ = bf16[65,16,384]{2,1,0:T(8,128)(2,1)S(1)} concatenate(bf16[65,2,384]{2,1,0:T(2,128)(2,1)S(1)} %get-tuple-element.114, bf16[65,2,384]{2,1,0:T(2,128)(2,1)S(1)} %get-tuple-element.112, bf16[65,4,384]{2,1,0:T(4,128)(2,1)S(1)} %collective-permute-done.4, bf16[65,4,384]{2,1,0:T(4,128)(2,1)S(1)} %collective-permute-done.5, ...), dimensions={1} | concatenate | bytes 1597440 | tf_op jit(solution)/shard_map/concatenate | solution.py:315
  45.9 1.5 collective-permute-done.9
  47.4 1.3 collective-permute-start.13
  48.8 1.4 collective-permute-start.11
  50.1 2.0 %collective-permute-done.13 = bf16[65,4,384]{2,1,0:T(4,128)(2,1)S(1)} collective-permute-done((bf16[65,4,384]{2,1,0:T(4,128)(2,1)}, bf16[65,4,384]{2,1,0:T(4,128)(2,1)S(1)}, u32[]{:S(2)}, u32[]{:S(2)}) %collective-permute-start.13) | collective-permute-done | bytes 199712 | tf_op jit(solution)/shard_map/ppermute | solution.py:28
  52.1 1.6 pad_maximum_fusion.2.refs_3_.refs_9_
  53.8 0.9 convert_element_type.95.refs_11_.refs_13_
  54.8 2.8 %copy-done = bf16[2,128,96,128]{3,2,1,0:T(8,128)(2,1)S(1)} copy-done((bf16[2,128,96,128]{3,2,1,0:T(8,128)(2,1)S(1)}, bf16[2,128,96,128]{3,2,1,0:T(8,128)(2,1)}, u32[]{:S(2)}) %copy-start) | copy-done | bytes 6291480
  57.6 2.9 %whiten_channels.1.refs_10_.refs_12_ = bf16[2,128,96,128]{3,2,1,0:T(8,128)(2,1)S(1)} custom-call(bf16[2,128,96,128]{3,2,1,0:T(8,128)(2,1)S(1)} %copy-done, bf16[96,128]{1,0:T(8,128)(2,1)S(1)} %constant_dynamic-slice_fusion.valid_ref), custom_call_target="tpu_custom_call" | custom-call | flops 1000000 | bytes 100000 | tf_op jit(solution)/shard_map/whiten_channels/pallas_call | solution.py:109
  60.5 8.0 %collective-permute-done.10.refs_1_.refs_6_ = bf16[65,16,384]{2,1,0:T(8,128)(2,1)S(1)} collective-permute-done((bf16[65,16,384]{2,1,0:T(8,128)(2,1)S(1)}, bf16[65,16,384]{2,1,0:T(8,128)(2,1)S(1)}, u32[]{:S(2)}, u32[]{:S(2)}) %collective-permute-start.10) | collective-permute-done | bytes 798752 | tf_op jit(solution)/shard_map/ppermute | solution.py:28
  68.4 3.5 %collective-permute-start.15 = (bf16[65,16,384]{2,1,0:T(8,128)(2,1)S(1)}, bf16[65,16,384]{2,1,0:T(8,128)(2,1)S(1)}, u32[]{:S(2)}, u32[]{:S(2)}) collective-permute-start(bf16[65,16,384]{2,1,0:T(8,128)(2,1)S(1)} %collective-permute-done.10.refs_1_.refs_6_), channel_id=1, source_target_pairs={{0,7},{1,0},{2,1},{3,2},{4,3},{5,4},{6,5},{7,6},{8,15},{9,8},{10,9... | collective-permute-start | bytes 2396168 | tf_op jit(solution)/shard_map/ppermute | solution.py:28
  72.0 1.5 collective-permute-start.18
  73.4 0.3 cosine_convert_fusion
  73.8 0.3 fusion.3
  74.1 8.0 %cross_lag.3 = (bf16[24,128,128]{2,1,0:T(8,128)(2,1)S(1)}, bf16[56,128,128]{2,1,0:T(8,128)(2,1)S(1)}, f32[80,128]{1,0:T(8,128)S(1)}) custom-call(bf16[65,16,384]{2,1,0:T(8,128)(2,1)S(1)} %pad_maximum_fusion.1.refs_0_.refs_5_, bf16[65,16,384]{2,1,0:T(8,128)(2,1)S(1)} %collective-permute-done.10.refs_1_.refs_6_, ...), custom_call_target="tpu_custom_call" | custom-call | flops 5000000 | bytes 500000 | tf_op jit(solution)/shard_map/cross_lag/pallas_call | solution.py:177
  82.1 1.1 collective-permute-done.15.refs_0_.refs_6_
  83.2 3.3 %collective-permute-done.16.refs_1_.refs_7_ = bf16[65,16,384]{2,1,0:T(8,128)(2,1)S(1)} collective-permute-done((bf16[65,16,384]{2,1,0:T(8,128)(2,1)}, bf16[65,16,384]{2,1,0:T(8,128)(2,1)S(1)}, u32[]{:S(2)}, u32[]{:S(2)}) %collective-permute-start.16) | collective-permute-done | bytes 798752 | tf_op jit(solution)/shard_map/ppermute | solution.py:28
  86.5 7.1 %collective-permute-start.23 = (bf16[56,128,128]{2,1,0:T(8,128)(2,1)S(1)}, bf16[56,128,128]{2,1,0:T(8,128)(2,1)S(1)}, u32[]{:S(2)}, u32[]{:S(2)}) collective-permute-start(bf16[56,128,128]{2,1,0:T(8,128)(2,1)S(1)} %get-tuple-element.72), channel_id=1, source_target_pairs={{0,64},{64,0},{1,65},{65,1},{2,66},{66,2},{3,67},{67,3},{4,68},{68... | collective-permute-start | bytes 5505032 | tf_op jit(solution)/shard_map/ppermute | solution.py:28
  93.6 2.7 %collective-permute-start.19 = (bf16[65,16,384]{2,1,0:T(8,128)(2,1)S(1)}, bf16[65,16,384]{2,1,0:T(8,128)(2,1)S(1)}, u32[]{:S(2)}, u32[]{:S(2)}) collective-permute-start(bf16[65,16,384]{2,1,0:T(8,128)(2,1)S(1)} %collective-permute-done.15.refs_0_.refs_6_), channel_id=1, source_target_pairs={{0,7},{1,0},{2,1},{3,2},{4,3},{5,4},{6,5},{7,6},{8,15},{9,8},{10,9... | collective-permute-start | bytes 2396168 | tf_op jit(solution)/shard_map/ppermute | solution.py:28
  96.3 1.5 collective-permute-start.22
  97.8 0.2 add_convert_fusion.5
  98.0 1.5 collective-permute-start.24
  99.5 0.4 add_convert_fusion.2
  99.9 6.1 %cross_lag.4 = (bf16[16,128,128]{2,1,0:T(8,128)(2,1)S(1)}, bf16[80,128,128]{2,1,0:T(8,128)(2,1)S(1)}, f32[96,128]{1,0:T(8,128)S(1)}) custom-call(bf16[65,16,384]{2,1,0:T(8,128)(2,1)S(1)} %collective-permute-done.15.refs_0_.refs_6_, bf16[65,16,384]{2,1,0:T(8,128)(2,1)S(1)} %collective-permute-done.16.refs_1_.refs_7_, ...), custom_call_target="tpu_custom_call" | custom-call | flops 6000000 | bytes 600000 | tf_op jit(solution)/shard_map/cross_lag/pallas_call | solution.py:177
  106.0 7.5 %collective-permute-done.19.refs_0_.refs_5_ = bf16[65,16,384]{2,1,0:T(8,128)(2,1)S(1)} collective-permute-done((bf16[65,16,384]{2,1,0:T(8,128)(2,1)S(1)}, bf16[65,16,384]{2,1,0:T(8,128)(2,1)S(1)}, u32[]{:S(2)}, u32[]{:S(2)}) %collective-permute-start.19) | collective-permute-done | bytes 798752 | tf_op jit(solution)/shard_map/ppermute | solution.py:28
  113.5 3.1 %collective-permute-done.20.refs_1_.refs_6_ = bf16[65,16,384]{2,1,0:T(8,128)(2,1)S(1)} collective-permute-done((bf16[65,16,384]{2,1,0:T(8,128)(2,1)S(1)}, bf16[65,16,384]{2,1,0:T(8,128)(2,1)S(1)}, u32[]{:S(2)}, u32[]{:S(2)}) %collective-permute-start.20) | collective-permute-done | bytes 798752 | tf_op jit(solution)/shard_map/ppermute | solution.py:28
  116.6 1.2 collective-permute-start.28
  117.9 2.7 %collective-permute-start.26 = (bf16[33,16,384]{2,1,0:T(8,128)(2,1)S(1)}, bf16[33,16,384]{2,1,0:T(8,128)(2,1)S(1)}, u32[]{:S(2)}, u32[]{:S(2)}) collective-permute-start(bf16[33,16,384]{2,1,0:T(8,128)(2,1)S(1)} %slice.181), channel_id=1, source_target_pairs={{0,7},{1,0},{2,1},{3,2},{4,3},{5,4},{6,5},{7,6},{8,15},{9,8},{10,9... | collective-permute-start | bytes 1216520 | tf_op jit(solution)/shard_map/ppermute | solution.py:28
  120.7 3.1 %collective-permute-start.27 = (bf16[16,128,128]{2,1,0:T(8,128)(2,1)S(1)}, bf16[16,128,128]{2,1,0:T(8,128)(2,1)S(1)}, u32[]{:S(2)}, u32[]{:S(2)}) collective-permute-start(bf16[16,128,128]{2,1,0:T(8,128)(2,1)S(1)} %get-tuple-element.106), channel_id=1, source_target_pairs={{64,192},{192,64},{16,144},{144,16},{96,224},{224,96},{48,176},{17... | collective-permute-start | bytes 1572872 | tf_op jit(solution)/shard_map/ppermute | solution.py:286
  123.8 8.5 %collective-permute-done.25 = bf16[32,16,384]{2,1,0:T(8,128)(2,1)S(1)} collective-permute-done((bf16[32,16,384]{2,1,0:T(8,128)(2,1)S(1)}, bf16[32,16,384]{2,1,0:T(8,128)(2,1)S(1)}, u32[]{:S(2)}, u32[]{:S(2)}) %collective-permute-start.25) | collective-permute-done | bytes 393248 | tf_op jit(solution)/shard_map/ppermute | solution.py:28
  132.6 1.2 collective-permute-start.29
  133.8 2.1 %add_convert_fusion = bf16[64,128,128]{2,1,0:T(8,128)(2,1)} fusion(bf16[80,128,128]{2,1,0:T(8,128)(2,1)S(1)} %collective-permute-done.28, bf16[80,128,128]{2,1,0:T(8,128)(2,1)S(1)} %get-tuple-element.83), kind=kLoop, calls=%fused_computation | loop fusion | flops 4194304 | bytes 6291456 | tf_op jit(solution)/shard_map/convert_element_type | solution.py:250
  135.9 3.5 %collective-permute-done.29.refs_4_ = bf16[8,128,128]{2,1,0:T(8,128)(2,1)S(1)} collective-permute-done((bf16[8,128,128]{2,1,0:T(8,128)(2,1)S(1)}, bf16[8,128,128]{2,1,0:T(8,128)(2,1)S(1)}, u32[]{:S(2)}, u32[]{:S(2)}) %collective-permute-start.29) | collective-permute-done | bytes 262176 | tf_op jit(solution)/shard_map/ppermute | solution.py:28
  139.3 6.7 %cross_lag.5 = (bf16[24,128,128]{2,1,0:T(8,128)(2,1)S(1)}, bf16[56,128,128]{2,1,0:T(8,128)(2,1)}, f32[80,128]{1,0:T(8,128)S(1)}) custom-call(bf16[65,16,384]{2,1,0:T(8,128)(2,1)S(1)} %collective-permute-done.19.refs_0_.refs_5_, bf16[65,16,384]{2,1,0:T(8,128)(2,1)S(1)} %collective-permute-done.20.refs_1_.refs_6_, ...), custom_call_target="tpu_custom_call" | custom-call | flops 5000000 | bytes 500000 | tf_op jit(solution)/shard_map/cross_lag/pallas_call | solution.py:177
  146.1 2.0 %collective-permute-start.30 = (bf16[56,128,128]{2,1,0:T(8,128)(2,1)}, bf16[56,128,128]{2,1,0:T(8,128)(2,1)}, u32[]{:S(2)}, u32[]{:S(2)}) collective-permute-start(bf16[56,128,128]{2,1,0:T(8,128)(2,1)} %get-tuple-element.91), channel_id=1, source_target_pairs={{0,64},{64,0},{1,65},{65,1},{2,66},{66,2},{3,67},{67,3},{4,68},{68... | collective-permute-start | bytes 5505032 | tf_op jit(solution)/shard_map/ppermute | solution.py:28
  148.3 1.7 broadcast_select_fusion
  150.0 0.7 collective-permute-start.32
  150.7 1.2 collective-permute-done.30
  151.9 1.9 %add_convert_fusion.1 = bf16[32,128,128]{2,1,0:T(8,128)(2,1)S(1)} fusion(bf16[56,128,128]{2,1,0:T(8,128)(2,1)} %collective-permute-done.30, bf16[56,128,128]{2,1,0:T(8,128)(2,1)} %get-tuple-element.91), kind=kLoop, calls=%fused_computation.1 | loop fusion | flops 2097152 | bytes 3145728 | tf_op jit(solution)/shard_map/convert_element_type | solution.py:250
  153.9 3.1 %collective-permute-start.33 = (bf16[16,128,128]{2,1,0:T(8,128)(2,1)S(1)}, bf16[16,128,128]{2,1,0:T(8,128)(2,1)S(1)}, u32[]{:S(2)}, u32[]{:S(2)}) collective-permute-start(bf16[16,128,128]{2,1,0:T(8,128)(2,1)S(1)} %get-tuple-element.104), channel_id=1, source_target_pairs={{64,192},{192,64},{16,144},{144,16},{96,224},{224,96},{48,176},{17... | collective-permute-start | bytes 1572872 | tf_op jit(solution)/shard_map/ppermute | solution.py:286
  156.9 1.3 add_convert_fusion.3
  158.3 0.4 collective-permute-start.31
  158.7 19.5 %collective-permute-done.31.refs_7_ = bf16[12,128,128]{2,1,0:T(8,128)(2,1)S(1)} collective-permute-done((bf16[12,128,128]{2,1,0:T(8,128)(2,1)S(1)}, bf16[12,128,128]{2,1,0:T(8,128)(2,1)S(1)}, u32[]{:S(2)}, u32[]{:S(2)}) %collective-permute-start.31) | collective-permute-done | bytes 393248 | tf_op jit(solution)/shard_map/ppermute | solution.py:28
  178.2 4.3 %finish_lags.1 = (bf16[64,128,128]{2,1,0:T(8,128)(2,1)}, f32[64,128]{1,0:T(8,128)}) custom-call(s32[96]{0:T(128)S(1)} %fusion.6.rows_ref, s32[6]{0:T(128)S(1)} %select_select_fusion.live_ref, s32[2,64,128]{2,1,0:T(8,128)S(1)} %pad_add_fusion.bounds_ref, bf16[12,128,128]{2,1,0:T(8,128)(2,1)S(1)} %get-tuple-element.76.refs_0_, ...), custom_call_target="tpu_custom_call" | custom-call | flops 10000000 | bytes 8000000 | tf_op jit(solution)/shard_map/finish_lags/pallas_call | solution.py:226
  (65 shorter events, 1.1 us)
Async XLA Ops:
  2.0 11.6 %copy-start.2 = (s32[96,3]{0,1:T(4,128)S(1)}, s32[96,3]{0,1:T(4,128)}, u32[]{:S(2)}) copy-start(s32[96,3]{0,1:T(4,128)} %constant.122.clone) | copy-start | bytes 3460
  2.0 11.6 %copy-start.3 = (s32[96,3]{0,1:T(4,128)S(1)}, s32[96,3]{0,1:T(4,128)}, u32[]{:S(2)}) copy-start(s32[96,3]{0,1:T(4,128)} %constant.123.clone) | copy-start | bytes 3460
  8.6 21.3 %copy-start.4 = (pred[6]{0:T(512)(128)(4,1)S(1)}, pred[6]{0:T(512)(128)(4,1)}, u32[]{:S(2)}) copy-start(pred[6]{0:T(512)(128)(4,1)} %constant.124.clone) | copy-start | bytes 22
  8.6 21.3 %copy-start.5 = (pred[6]{0:T(512)(128)(4,1)S(1)}, pred[6]{0:T(512)(128)(4,1)}, u32[]{:S(2)}) copy-start(pred[6]{0:T(512)(128)(4,1)} %constant.125.clone) | copy-start | bytes 22
  8.7 7.6 %collective-permute-start = (bf16[65,4,384]{2,1,0:T(4,128)(2,1)}, bf16[65,4,384]{2,1,0:T(4,128)(2,1)S(1)}, u32[]{:S(2)}, u32[]{:S(2)}) collective-permute-start(bf16[65,4,384]{2,1,0:T(4,128)(2,1)} %pick_sources.1), channel_id=1, source_target_pairs={{0,8},{8,0},{1,9},{9,1},{2,10},{10,2},{3,11},{11,3},{4,12},{12,4},... | collective-permute-start | bytes 599048 | tf_op jit(solution)/shard_map/ppermute | solution.py:28
  16.6 10.6 %collective-permute-start.4 = (bf16[65,4,384]{2,1,0:T(4,128)(2,1)S(1)}, bf16[65,4,384]{2,1,0:T(4,128)(2,1)S(1)}, u32[]{:S(2)}, u32[]{:S(2)}) collective-permute-start(bf16[65,4,384]{2,1,0:T(4,128)(2,1)S(1)} %pad_maximum_fusion.5), channel_id=1, source_target_pairs={{0,7},{1,0},{2,1},{3,2},{4,3},{5,4},{6,5},{7,6},{8,15},{9,8},{10,9... | collective-permute-start | bytes 599048 | tf_op jit(solution)/shard_map/ppermute | solution.py:28
  23.1 6.8 %collective-permute-start.5 = (bf16[65,4,384]{2,1,0:T(4,128)(2,1)S(1)}, bf16[65,4,384]{2,1,0:T(4,128)(2,1)S(1)}, u32[]{:S(2)}, u32[]{:S(2)}) collective-permute-start(bf16[65,4,384]{2,1,0:T(4,128)(2,1)S(1)} %pad_maximum_fusion.5), channel_id=1, source_target_pairs={{0,1},{1,2},{2,3},{3,4},{4,5},{5,6},{6,7},{7,0},{8,9},{9,10},{10,1... | collective-permute-start | bytes 599048 | tf_op jit(solution)/shard_map/ppermute | solution.py:28
  23.4 7.4 %collective-permute-start.1 = (bf16[65,4,384]{2,1,0:T(4,128)(2,1)S(1)}, bf16[65,4,384]{2,1,0:T(4,128)(2,1)S(1)}, u32[]{:S(2)}, u32[]{:S(2)}) collective-permute-start(bf16[65,4,384]{2,1,0:T(4,128)(2,1)S(1)} %get-tuple-element.117), channel_id=1, source_target_pairs={{0,48},{16,0},{32,16},{48,32},{1,49},{17,1},{33,17},{49,33},{2,50}... | collective-permute-start | bytes 599048 | tf_op jit(solution)/shard_map/ppermute | solution.py:28
  26.2 6.2 %collective-permute-start.2 = (bf16[65,4,384]{2,1,0:T(4,128)(2,1)S(1)}, bf16[65,4,384]{2,1,0:T(4,128)(2,1)S(1)}, u32[]{:S(2)}, u32[]{:S(2)}) collective-permute-start(bf16[65,4,384]{2,1,0:T(4,128)(2,1)S(1)} %get-tuple-element.117), channel_id=1, source_target_pairs={{0,32},{16,48},{32,0},{48,16},{1,33},{17,49},{33,1},{49,17},{2,34}... | collective-permute-start | bytes 599048 | tf_op jit(solution)/shard_map/ppermute | solution.py:28
  26.6 11.7 %collective-permute-start.3 = (bf16[65,4,384]{2,1,0:T(4,128)(2,1)S(1)}, bf16[65,4,384]{2,1,0:T(4,128)(2,1)S(1)}, u32[]{:S(2)}, u32[]{:S(2)}) collective-permute-start(bf16[65,4,384]{2,1,0:T(4,128)(2,1)S(1)} %get-tuple-element.117), channel_id=1, source_target_pairs={{0,16},{16,32},{32,48},{48,0},{1,17},{17,33},{33,49},{49,1},{2,18}... | collective-permute-start | bytes 599048 | tf_op jit(solution)/shard_map/ppermute | solution.py:28
  27.3 11.8 %collective-permute-start.6 = (bf16[65,4,384]{2,1,0:T(4,128)(2,1)S(1)}, bf16[65,4,384]{2,1,0:T(4,128)(2,1)}, u32[]{:S(2)}, u32[]{:S(2)}) collective-permute-start(bf16[65,4,384]{2,1,0:T(4,128)(2,1)S(1)} %collective-permute-done.4), channel_id=1, source_target_pairs={{0,7},{1,0},{2,1},{3,2},{4,3},{5,4},{6,5},{7,6},{8,15},{9,8},{10,9... | collective-permute-start | bytes 599048 | tf_op jit(solution)/shard_map/ppermute | solution.py:28
  29.9 11.6 %collective-permute-start.7 = (bf16[65,4,384]{2,1,0:T(4,128)(2,1)S(1)}, bf16[65,4,384]{2,1,0:T(4,128)(2,1)S(1)}, u32[]{:S(2)}, u32[]{:S(2)}) collective-permute-start(bf16[65,4,384]{2,1,0:T(4,128)(2,1)S(1)} %collective-permute-done.5), channel_id=1, source_target_pairs={{0,1},{1,2},{2,3},{3,4},{4,5},{5,6},{6,7},{7,0},{8,9},{9,10},{10,1... | collective-permute-start | bytes 599048 | tf_op jit(solution)/shard_map/ppermute | solution.py:28
  39.0 6.9 %collective-permute-start.8 = (bf16[65,4,384]{2,1,0:T(4,128)(2,1)}, bf16[65,4,384]{2,1,0:T(4,128)(2,1)}, u32[]{:S(2)}, u32[]{:S(2)}) collective-permute-start(bf16[65,4,384]{2,1,0:T(4,128)(2,1)} %collective-permute-done.6), channel_id=1, source_target_pairs={{0,7},{1,0},{2,1},{3,2},{4,3},{5,4},{6,5},{7,6},{8,15},{9,8},{10,9... | collective-permute-start | bytes 599048 | tf_op jit(solution)/shard_map/ppermute | solution.py:28
  41.5 5.9 %collective-permute-start.9 = (bf16[65,4,384]{2,1,0:T(4,128)(2,1)S(1)}, bf16[65,4,384]{2,1,0:T(4,128)(2,1)}, u32[]{:S(2)}, u32[]{:S(2)}) collective-permute-start(bf16[65,4,384]{2,1,0:T(4,128)(2,1)S(1)} %collective-permute-done.7), channel_id=1, source_target_pairs={{0,1},{1,2},{2,3},{3,4},{4,5},{5,6},{6,7},{7,0},{8,9},{9,10},{10,1... | collective-permute-start | bytes 599048 | tf_op jit(solution)/shard_map/ppermute | solution.py:28
  47.4 4.8 %collective-permute-start.13 = (bf16[65,4,384]{2,1,0:T(4,128)(2,1)}, bf16[65,4,384]{2,1,0:T(4,128)(2,1)S(1)}, u32[]{:S(2)}, u32[]{:S(2)}) collective-permute-start(bf16[65,4,384]{2,1,0:T(4,128)(2,1)} %collective-permute-done.8), channel_id=1, source_target_pairs={{0,7},{1,0},{2,1},{3,2},{4,3},{5,4},{6,5},{7,6},{8,15},{9,8},{10,9... | collective-permute-start | bytes 599048 | tf_op jit(solution)/shard_map/ppermute | solution.py:28
  48.7 19.8 %collective-permute-start.10 = (bf16[65,16,384]{2,1,0:T(8,128)(2,1)S(1)}, bf16[65,16,384]{2,1,0:T(8,128)(2,1)S(1)}, u32[]{:S(2)}, u32[]{:S(2)}) collective-permute-start(bf16[65,16,384]{2,1,0:T(8,128)(2,1)S(1)} %pad_maximum_fusion.1.refs_0_.refs_5_), channel_id=1, source_target_pairs={{0,7},{1,0},{2,1},{3,2},{4,3},{5,4},{6,5},{7,6},{8,15},{9,8},{10,9... | collective-permute-start | bytes 2396168 | tf_op jit(solution)/shard_map/ppermute | solution.py:28
  48.8 19.7 %collective-permute-start.11 = (bf16[65,16,384]{2,1,0:T(8,128)(2,1)S(1)}, bf16[65,16,384]{2,1,0:T(8,128)(2,1)}, u32[]{:S(2)}, u32[]{:S(2)}) collective-permute-start(bf16[65,16,384]{2,1,0:T(8,128)(2,1)S(1)} %pad_maximum_fusion.1.refs_0_.refs_5_), channel_id=1, source_target_pairs={{0,1},{1,2},{2,3},{3,4},{4,5},{5,6},{6,7},{7,0},{8,9},{9,10},{10,1... | collective-permute-start | bytes 2396168 | tf_op jit(solution)/shard_map/ppermute | solution.py:28
  50.1 18.3 %collective-permute-start.12 = (bf16[65,16,384]{2,1,0:T(8,128)(2,1)S(1)}, bf16[65,16,384]{2,1,0:T(8,128)(2,1)}, u32[]{:S(2)}, u32[]{:S(2)}) collective-permute-start(bf16[65,16,384]{2,1,0:T(8,128)(2,1)S(1)} %concatenate.38.refs_2_.refs_8_), channel_id=1, source_target_pairs={{0,48},{16,0},{32,16},{48,32},{1,49},{17,1},{33,17},{49,33},{2,50}... | collective-permute-start | bytes 2396168 | tf_op jit(solution)/shard_map/ppermute | solution.py:28
  53.7 14.7 %collective-permute-start.14 = (bf16[65,16,384]{2,1,0:T(8,128)(2,1)S(1)}, bf16[65,16,384]{2,1,0:T(8,128)(2,1)}, u32[]{:S(2)}, u32[]{:S(2)}) collective-permute-start(bf16[65,16,384]{2,1,0:T(8,128)(2,1)S(1)} %pad_maximum_fusion.2.refs_3_.refs_9_), channel_id=1, source_target_pairs={{0,16},{16,32},{32,48},{48,0},{1,17},{17,33},{33,49},{49,1},{2,18}... | collective-permute-start | bytes 2396168 | tf_op jit(solution)/shard_map/ppermute | solution.py:28
  54.8 2.8 %copy-start = (bf16[2,128,96,128]{3,2,1,0:T(8,128)(2,1)S(1)}, bf16[2,128,96,128]{3,2,1,0:T(8,128)(2,1)}, u32[]{:S(2)}) copy-start(bf16[2,128,96,128]{3,2,1,0:T(8,128)(2,1)} %spec_ref.1) | copy-start | bytes 18874372
  68.4 14.8 %collective-permute-start.15 = (bf16[65,16,384]{2,1,0:T(8,128)(2,1)S(1)}, bf16[65,16,384]{2,1,0:T(8,128)(2,1)S(1)}, u32[]{:S(2)}, u32[]{:S(2)}) collective-permute-start(bf16[65,16,384]{2,1,0:T(8,128)(2,1)S(1)} %collective-permute-done.10.refs_1_.refs_6_), channel_id=1, source_target_pairs={{0,7},{1,0},{2,1},{3,2},{4,3},{5,4},{6,5},{7,6},{8,15},{9,8},{10,9... | collective-permute-start | bytes 2396168 | tf_op jit(solution)/shard_map/ppermute | solution.py:28
  72.0 14.6 %collective-permute-start.16 = (bf16[65,16,384]{2,1,0:T(8,128)(2,1)}, bf16[65,16,384]{2,1,0:T(8,128)(2,1)S(1)}, u32[]{:S(2)}, u32[]{:S(2)}) collective-permute-start(bf16[65,16,384]{2,1,0:T(8,128)(2,1)} %collective-permute-done.11.refs_2_.refs_7_), channel_id=1, source_target_pairs={{0,1},{1,2},{2,3},{3,4},{4,5},{5,6},{6,7},{7,0},{8,9},{9,10},{10,1... | collective-permute-start | bytes 2396168 | tf_op jit(solution)/shard_map/ppermute | solution.py:28
  72.0 14.6 %collective-permute-start.17 = (bf16[65,16,384]{2,1,0:T(8,128)(2,1)}, bf16[65,16,384]{2,1,0:T(8,128)(2,1)S(1)}, u32[]{:S(2)}, u32[]{:S(2)}) collective-permute-start(bf16[65,16,384]{2,1,0:T(8,128)(2,1)} %collective-permute-done.12.refs_3_.refs_8_), channel_id=1, source_target_pairs={{0,48},{16,0},{32,16},{48,32},{1,49},{17,1},{33,17},{49,33},{2,50}... | collective-permute-start | bytes 2396168 | tf_op jit(solution)/shard_map/ppermute | solution.py:28
  72.0 14.6 %collective-permute-start.18 = (bf16[65,16,384]{2,1,0:T(8,128)(2,1)}, bf16[65,16,384]{2,1,0:T(8,128)(2,1)S(1)}, u32[]{:S(2)}, u32[]{:S(2)}) collective-permute-start(bf16[65,16,384]{2,1,0:T(8,128)(2,1)} %collective-permute-done.14.refs_4_.refs_9_), channel_id=1, source_target_pairs={{0,16},{16,32},{32,48},{48,0},{1,17},{17,33},{33,49},{49,1},{2,18}... | collective-permute-start | bytes 2396168 | tf_op jit(solution)/shard_map/ppermute | solution.py:28
  86.5 11.2 %collective-permute-start.23 = (bf16[56,128,128]{2,1,0:T(8,128)(2,1)S(1)}, bf16[56,128,128]{2,1,0:T(8,128)(2,1)S(1)}, u32[]{:S(2)}, u32[]{:S(2)}) collective-permute-start(bf16[56,128,128]{2,1,0:T(8,128)(2,1)S(1)} %get-tuple-element.72), channel_id=1, source_target_pairs={{0,64},{64,0},{1,65},{65,1},{2,66},{66,2},{3,67},{67,3},{4,68},{68... | collective-permute-start | bytes 5505032 | tf_op jit(solution)/shard_map/ppermute | solution.py:28
  93.6 19.9 %collective-permute-start.19 = (bf16[65,16,384]{2,1,0:T(8,128)(2,1)S(1)}, bf16[65,16,384]{2,1,0:T(8,128)(2,1)S(1)}, u32[]{:S(2)}, u32[]{:S(2)}) collective-permute-start(bf16[65,16,384]{2,1,0:T(8,128)(2,1)S(1)} %collective-permute-done.15.refs_0_.refs_6_), channel_id=1, source_target_pairs={{0,7},{1,0},{2,1},{3,2},{4,3},{5,4},{6,5},{7,6},{8,15},{9,8},{10,9... | collective-permute-start | bytes 2396168 | tf_op jit(solution)/shard_map/ppermute | solution.py:28
  96.3 20.3 %collective-permute-start.20 = (bf16[65,16,384]{2,1,0:T(8,128)(2,1)S(1)}, bf16[65,16,384]{2,1,0:T(8,128)(2,1)S(1)}, u32[]{:S(2)}, u32[]{:S(2)}) collective-permute-start(bf16[65,16,384]{2,1,0:T(8,128)(2,1)S(1)} %collective-permute-done.16.refs_1_.refs_7_), channel_id=1, source_target_pairs={{0,1},{1,2},{2,3},{3,4},{4,5},{5,6},{6,7},{7,0},{8,9},{9,10},{10,1... | collective-permute-start | bytes 2396168 | tf_op jit(solution)/shard_map/ppermute | solution.py:28
  96.3 20.3 %collective-permute-start.21 = (bf16[65,16,384]{2,1,0:T(8,128)(2,1)S(1)}, bf16[65,16,384]{2,1,0:T(8,128)(2,1)S(1)}, u32[]{:S(2)}, u32[]{:S(2)}) collective-permute-start(bf16[65,16,384]{2,1,0:T(8,128)(2,1)S(1)} %collective-permute-done.17.refs_4_.refs_10_), channel_id=1, source_target_pairs={{0,48},{16,0},{32,16},{48,32},{1,49},{17,1},{33,17},{49,33},{2,50}... | collective-permute-start | bytes 2396168 | tf_op jit(solution)/shard_map/ppermute | solution.py:28
  96.3 20.3 %collective-permute-start.22 = (bf16[65,16,384]{2,1,0:T(8,128)(2,1)S(1)}, bf16[65,16,384]{2,1,0:T(8,128)(2,1)S(1)}, u32[]{:S(2)}, u32[]{:S(2)}) collective-permute-start(bf16[65,16,384]{2,1,0:T(8,128)(2,1)S(1)} %collective-permute-done.18.refs_5_.refs_11_), channel_id=1, source_target_pairs={{0,16},{16,32},{32,48},{48,0},{1,17},{17,33},{33,49},{49,1},{2,18}... | collective-permute-start | bytes 2396168 | tf_op jit(solution)/shard_map/ppermute | solution.py:28
  98.0 18.6 %collective-permute-start.24 = (bf16[12,128,128]{2,1,0:T(8,128)(2,1)S(1)}, bf16[12,128,128]{2,1,0:T(8,128)(2,1)S(1)}, u32[]{:S(2)}, u32[]{:S(2)}) collective-permute-start(bf16[12,128,128]{2,1,0:T(8,128)(2,1)S(1)} %get-tuple-element.100), channel_id=1, source_target_pairs={{0,128},{128,0},{1,129},{129,1},{2,130},{130,2},{3,131},{131,3},{4... | collective-permute-start | bytes 1179656 | tf_op jit(solution)/shard_map/ppermute | solution.py:28
  116.6 15.8 %collective-permute-start.28 = (bf16[80,128,128]{2,1,0:T(8,128)(2,1)S(1)}, bf16[80,128,128]{2,1,0:T(8,128)(2,1)S(1)}, u32[]{:S(2)}, u32[]{:S(2)}) collective-permute-start(bf16[80,128,128]{2,1,0:T(8,128)(2,1)S(1)} %get-tuple-element.83), channel_id=1, source_target_pairs={{0,64},{64,0},{1,65},{65,1},{2,66},{66,2},{3,67},{67,3},{4,68},{68... | collective-permute-start | bytes 7864328 | tf_op jit(solution)/shard_map/ppermute | solution.py:28
  117.9 14.4 %collective-permute-start.26 = (bf16[33,16,384]{2,1,0:T(8,128)(2,1)S(1)}, bf16[33,16,384]{2,1,0:T(8,128)(2,1)S(1)}, u32[]{:S(2)}, u32[]{:S(2)}) collective-permute-start(bf16[33,16,384]{2,1,0:T(8,128)(2,1)S(1)} %slice.181), channel_id=1, source_target_pairs={{0,7},{1,0},{2,1},{3,2},{4,3},{5,4},{6,5},{7,6},{8,15},{9,8},{10,9... | collective-permute-start | bytes 1216520 | tf_op jit(solution)/shard_map/ppermute | solution.py:28
  120.6 11.7 %collective-permute-start.25 = (bf16[32,16,384]{2,1,0:T(8,128)(2,1)S(1)}, bf16[32,16,384]{2,1,0:T(8,128)(2,1)S(1)}, u32[]{:S(2)}, u32[]{:S(2)}) collective-permute-start(bf16[32,16,384]{2,1,0:T(8,128)(2,1)S(1)} %slice.180), channel_id=1, source_target_pairs={{0,1},{1,2},{2,3},{3,4},{4,5},{5,6},{6,7},{7,0},{8,9},{9,10},{10,1... | collective-permute-start | bytes 1179656 | tf_op jit(solution)/shard_map/ppermute | solution.py:28
  120.7 15.1 %collective-permute-start.27 = (bf16[16,128,128]{2,1,0:T(8,128)(2,1)S(1)}, bf16[16,128,128]{2,1,0:T(8,128)(2,1)S(1)}, u32[]{:S(2)}, u32[]{:S(2)}) collective-permute-start(bf16[16,128,128]{2,1,0:T(8,128)(2,1)S(1)} %get-tuple-element.106), channel_id=1, source_target_pairs={{64,192},{192,64},{16,144},{144,16},{96,224},{224,96},{48,176},{17... | collective-permute-start | bytes 1572872 | tf_op jit(solution)/shard_map/ppermute | solution.py:286
  132.6 6.8 %collective-permute-start.29 = (bf16[8,128,128]{2,1,0:T(8,128)(2,1)S(1)}, bf16[8,128,128]{2,1,0:T(8,128)(2,1)S(1)}, u32[]{:S(2)}, u32[]{:S(2)}) collective-permute-start(bf16[8,128,128]{2,1,0:T(8,128)(2,1)S(1)} %get-tuple-element.96), channel_id=1, source_target_pairs={{0,128},{128,0},{1,129},{129,1},{2,130},{130,2},{3,131},{131,3},{4... | collective-permute-start | bytes 786440 | tf_op jit(solution)/shard_map/ppermute | solution.py:28
  139.3 8.8 %copy-start.1 = (s32[64,128,2]{1,2,0:T(2,128)S(1)}, s32[64,128,2]{1,2,0:T(2,128)}, u32[]{:S(2)}) copy-start(s32[64,128,2]{1,2,0:T(2,128)} %param.11) | copy-start | bytes 196612
  146.1 5.8 %collective-permute-start.30 = (bf16[56,128,128]{2,1,0:T(8,128)(2,1)}, bf16[56,128,128]{2,1,0:T(8,128)(2,1)}, u32[]{:S(2)}, u32[]{:S(2)}) collective-permute-start(bf16[56,128,128]{2,1,0:T(8,128)(2,1)} %get-tuple-element.91), channel_id=1, source_target_pairs={{0,64},{64,0},{1,65},{65,1},{2,66},{66,2},{3,67},{67,3},{4,68},{68... | collective-permute-start | bytes 5505032 | tf_op jit(solution)/shard_map/ppermute | solution.py:28
  150.0 8.7 %collective-permute-start.32 = (bf16[32,128,128]{2,1,0:T(8,128)(2,1)S(1)}, bf16[32,128,128]{2,1,0:T(8,128)(2,1)S(1)}, u32[]{:S(2)}, u32[]{:S(2)}) collective-permute-start(bf16[32,128,128]{2,1,0:T(8,128)(2,1)S(1)} %get-tuple-element.102), channel_id=1, source_target_pairs={{0,128},{128,0},{80,208},{208,80},{32,160},{160,32},{112,240},{240... | collective-permute-start | bytes 3145736 | tf_op jit(solution)/shard_map/ppermute | solution.py:286
  153.9 24.3 %collective-permute-start.33 = (bf16[16,128,128]{2,1,0:T(8,128)(2,1)S(1)}, bf16[16,128,128]{2,1,0:T(8,128)(2,1)S(1)}, u32[]{:S(2)}, u32[]{:S(2)}) collective-permute-start(bf16[16,128,128]{2,1,0:T(8,128)(2,1)S(1)} %get-tuple-element.104), channel_id=1, source_target_pairs={{64,192},{192,64},{16,144},{144,16},{96,224},{224,96},{48,176},{17... | collective-permute-start | bytes 1572872 | tf_op jit(solution)/shard_map/ppermute | solution.py:286
  158.3 19.9 %collective-permute-start.31 = (bf16[12,128,128]{2,1,0:T(8,128)(2,1)S(1)}, bf16[12,128,128]{2,1,0:T(8,128)(2,1)S(1)}, u32[]{:S(2)}, u32[]{:S(2)}) collective-permute-start(bf16[12,128,128]{2,1,0:T(8,128)(2,1)S(1)} %get-tuple-element.98), channel_id=1, source_target_pairs={{0,128},{128,0},{1,129},{129,1},{2,130},{130,2},{3,131},{131,3},{4... | collective-permute-start | bytes 1179656 | tf_op jit(solution)/shard_map/ppermute | solution.py:28
